TPU v7x, 32 devices: a whole 2x2x4 slice. The times are simulated.
32 devices in a mesh: seq: 4 (over z), tp: 4 (over y, x), fsdp: 2 (over core).
Axes of the slice: x: 2, y: 2, z: 4, core: 2. Of those that a mesh axis runs over, the one named last changes fastest.
Arguments:
- decoder_in: bfloat16 [32, 128, 1024], P(('seq', 'fsdp')), may hold values from -6 to 6
- memory: bfloat16 [32, 2048, 1024], P(('seq', 'fsdp')), may hold values from -6 to 6
- buckets: int32 [128, 128], replicated, may hold values from 0 to 31
- norm_gains: bfloat16 [3, 1024], P(None, ('seq', 'fsdp')), may hold values from 0.5 to 1.5
- rel_bias: bfloat16 [32, 16], P(('seq', 'fsdp'), 'tp'), may hold values from -4 to 4
- self_q: bfloat16 [1024, 1024], P(('seq', 'fsdp'), 'tp'), may hold values from -0.1875 to 0.1875
- self_kv: bfloat16 [1024, 2, 512], P(('seq', 'fsdp'), None, 'tp'), may hold values from -0.1875 to 0.1875
- self_out: bfloat16 [1024, 1024], P('tp', ('seq', 'fsdp')), may hold values from -0.75 to 0.75
- cross_q: bfloat16 [1024, 1024], P(('seq', 'fsdp'), 'tp'), may hold values from -0.1875 to 0.1875
- cross_kv: bfloat16 [1024, 2, 512], P(('seq', 'fsdp'), None, 'tp'), may hold values from -0.1875 to 0.1875
- cross_out: bfloat16 [1024, 1024], P('tp', ('seq', 'fsdp')), may hold values from -3 to 3
- gate_up: bfloat16 [1024, 2, 2816], P(('seq', 'fsdp'), None, 'tp'), may hold values from -0.1875 to 0.1875
- down: bfloat16 [2816, 1024], P('tp', ('seq', 'fsdp')), may hold values from -0.109375 to 0.109375
- cotangent: bfloat16 [32, 128, 1024], P(('seq', 'fsdp')), may hold values from -6 to 6
Outputs:
- decoder_out: bfloat16 [32, 128, 1024], P(('seq', 'fsdp'))
- decoder_grad: float32 [32, 128, 1024], P(('seq', 'fsdp'))
- memory_grad: bfloat16 [32, 2048, 1024], P(('seq', 'fsdp'), None, 'tp')
- gains_grad: float32 [3, 1024], P(None, ('seq', 'fsdp'))
- bias_grad: float32 [32, 16], P(('seq', 'fsdp'), 'tp')
- self_q_grad: float32 [1024, 1024], P(('seq', 'fsdp'), 'tp')
- self_kv_grad: float32 [1024, 2, 512], P(('seq', 'fsdp'), None, 'tp')
- self_out_grad: float32 [1024, 1024], P('tp', ('seq', 'fsdp'))
- cross_q_grad: float32 [1024, 1024], P(('seq', 'fsdp'), 'tp')
- cross_kv_grad: float32 [1024, 2, 512], P(('seq', 'fsdp'), None, 'tp')
- cross_out_grad: float32 [1024, 1024], P('tp', ('seq', 'fsdp'))
- gate_up_grad: float32 [1024, 2, 2816], P(('seq', 'fsdp'), None, 'tp')
- down_grad: float32 [2816, 1024], P('tp', ('seq', 'fsdp'))
Inputs may be any that keep to these rules, and one draw needn't show every extreme that they name: `buckets`: the bucket of query position i and key position j, the same for every sequence and head.
All inputs are finite; a program needn't handle non-finite values.
Results may differ from a plain program's by a relative error of at most 0.04.
Values may be sent and summed in bfloat16 or wider, within the bound.
No kernel may reach another device: no remote copies, remote signals or barrier semaphores. Data moves between devices by JAX's collectives and lax.ppermute only.
A program may use at most 192 MiB of HBM per device.

v0:
```python
import jax
import jax.numpy as jnp
from jax import lax
from jax.sharding import PartitionSpec as P

DH = 64
NB = 32
EPSILON = 1e-06
MASKED = -1e30
F32 = jnp.float32
BF16 = jnp.bfloat16


def rms_norm(values, gain):
    return values * lax.rsqrt(jnp.mean(values * values, axis=-1, keepdims=True) + EPSILON) * gain


def gelu_product(gate, up):
    return jax.nn.gelu(gate, approximate=True) * up


def mm(a, b, dims):
    return lax.dot_general(a, b, (dims, ((), ())), preferred_element_type=F32)


def split_heads(query, keys, values):
    batch, rows, width = query.shape
    span = keys.shape[1]
    groups = keys.shape[2] // DH
    ratio = width // DH // groups
    return (
        query.reshape(batch, rows, groups, ratio, DH),
        keys.reshape(batch, span, groups, DH),
        values.reshape(batch, span, groups, DH),
    )


def scores_of(query_heads, key_heads, bias, causal):
    scores = jnp.einsum(
        "bigrd,bjgd->bgrij", query_heads, key_heads, preferred_element_type=F32
    ) * DH ** (-0.5)
    if bias is not None:
        scores = scores + bias
    if causal is not None:
        scores = jnp.where(causal, scores, MASKED)
    return scores


def attend_forward(query, keys, values, bias, causal):
    query_heads, key_heads, value_heads = split_heads(query, keys, values)
    scores = scores_of(query_heads, key_heads, bias, causal)
    row_max = jnp.max(scores, axis=-1, keepdims=True)
    exponent = jnp.exp(scores - row_max)
    total = jnp.sum(exponent, axis=-1, keepdims=True)
    probs = (exponent / total).astype(BF16)
    mixed = jnp.einsum("bgrij,bjgd->bigrd", probs, value_heads, preferred_element_type=F32)
    return (mixed.reshape(query.shape).astype(BF16), row_max + jnp.log(total))


def attend_backward(query, keys, values, bias, causal, log_total, grad_mixed):
    query_heads, key_heads, value_heads = split_heads(query, keys, values)
    probs = jnp.exp(scores_of(query_heads, key_heads, bias, causal) - log_total)
    grad_heads = grad_mixed.reshape(query_heads.shape)
    grad_probs = jnp.einsum(
        "bigrd,bjgd->bgrij", grad_heads, value_heads, preferred_element_type=F32
    )
    inner = jnp.sum(probs * grad_probs, axis=-1, keepdims=True)
    grad_scores = (probs * (grad_probs - inner)).astype(BF16)
    scale = DH ** (-0.5)
    grad_query = (
        jnp.einsum("bgrij,bjgd->bigrd", grad_scores, key_heads, preferred_element_type=F32) * scale
    ).astype(BF16)
    grad_keys = (
        jnp.einsum("bgrij,bigrd->bjgd", grad_scores, query_heads, preferred_element_type=F32)
        * scale
    ).astype(BF16)
    grad_values = jnp.einsum(
        "bgrij,bigrd->bjgd", probs.astype(BF16), grad_heads, preferred_element_type=F32
    ).astype(BF16)
    return (
        grad_query.reshape(query.shape),
        grad_keys.reshape(keys.shape),
        grad_values.reshape(values.shape),
        grad_scores,
    )


def per_device(
    decoder_in,
    memory,
    buckets,
    norm_gains,
    rel_bias,
    self_q,
    self_kv,
    self_out,
    cross_q,
    cross_kv,
    cross_out,
    gate_up,
    down,
    cotangent,
    tp_size,
    seq_size,
):
    batch, rows, width = decoder_in.shape
    split = tp_size // batch
    if batch * split != tp_size or rows % split:
        raise ValueError("unsupported mesh")
    chunk = rows // split
    t = lax.axis_index("tp")
    f = lax.axis_index("fsdp")
    s = lax.axis_index("seq")
    zf = ("seq", "fsdp")

    def swap_tp(x, j):
        return lax.ppermute(x, "tp", [(i, i ^ j) for i in range(tp_size)])

    def swap_core(x):
        return lax.ppermute(x, "fsdp", [(0, 1), (1, 0)])

    def exchange(pieces):
        return [pieces[0]] + [swap_tp(pieces[j], j) for j in range(1, tp_size)]

    def spread(x):
        return [x] + [swap_tp(x, j) for j in range(1, tp_size)]

    def relative(x, member, count):
        return jnp.stack([lax.dynamic_index_in_dim(x, member ^ j, 0, False) for j in range(count)])

    def piece(x, j):
        part = x[j // split]
        if split == 1:
            return part
        return lax.dynamic_slice_in_dim(part, (t % split ^ j % split) * chunk, chunk, 0)

    def pieces_of(x):
        return [piece(x, j) for j in range(tp_size)]

    def whole_rows(pieces):
        if split == 1:
            return jnp.stack(pieces)
        out = []
        for b in range(batch):
            own = jnp.stack(pieces[b * split : (b + 1) * split])
            own = relative(own, t % split, split)
            out.append(own.reshape((rows,) + own.shape[2:]))
        return jnp.stack(out)

    def placed(pieces):
        out = jnp.zeros((tp_size,) + pieces[0].shape, pieces[0].dtype)
        for j in range(tp_size):
            out = lax.dynamic_update_index_in_dim(out, pieces[j], t ^ j, 0)
        return out

    def rejoin(own, other):
        first = jnp.where(f == 0, own, other)
        second = jnp.where(f == 0, other, own)
        full = jnp.stack([first, second], axis=1)
        return full.reshape(-1, full.shape[-1])

    shard = self_q.shape[0]
    extra = jnp.zeros((4, shard), BF16)
    extra = extra.at[:3].set(norm_gains)
    tb_rows, heads = rel_bias.shape
    extra = extra.at[3, : tb_rows * heads].set(rel_bias.reshape(-1))
    extra = lax.all_gather(extra, zf, axis=0, tiled=False)
    gains = jnp.transpose(extra[:, :3], (1, 0, 2)).reshape(3, -1).astype(F32)
    table = extra[:, 3, : tb_rows * heads].reshape(NB, heads)
    pack_full = jnp.stack(
        [
            jnp.concatenate([self_out.T, cross_kv.reshape(shard, -1)], axis=1),
            jnp.concatenate([cross_q, cross_out.T], axis=1),
        ]
    )
    got_full = lax.all_gather(pack_full, "seq", axis=0, tiled=False)
    pack_self = jnp.concatenate([self_q, self_kv.reshape(shard, -1)], axis=1)
    w_self = lax.all_gather(pack_self, zf, axis=0, tiled=True)
    pack_ffn = jnp.concatenate([gate_up.reshape(shard, -1), down.T], axis=1)
    w_ffn = lax.all_gather(pack_ffn, zf, axis=0, tiled=True)
    cols = self_q.shape[1]

    def full_pair(index):
        part = got_full[:, index]
        mine = spread(part)
        theirs = [swap_core(p) for p in mine]
        joined = [rejoin(a, b) for a, b in zip(mine, theirs)]
        first = jnp.concatenate([w[:, :cols] for w in joined], axis=1)
        second = jnp.concatenate([w[:, cols:] for w in joined], axis=1)
        return (first, second)

    w_so, w_ckv = full_pair(0)
    w_cq, w_co = full_pair(1)
    positions = jnp.arange(rows, dtype=jnp.int32)
    causal = positions[:, None] >= positions[None, :]
    onehot = (buckets[:, :, None] == jnp.arange(NB, dtype=jnp.int32)[None, None, :]).astype(BF16)
    kv_half = self_kv.shape[2]
    groups = kv_half // DH
    bias = jnp.einsum("ijn,nh->hij", onehot, table, preferred_element_type=F32).reshape(
        groups, heads // groups, rows, rows
    )
    tokens = relative(decoder_in, t // split, batch)
    start = tokens.astype(F32)
    normed_self = rms_norm(start, gains[0]).astype(BF16)
    proj = mm(normed_self, w_self, ((2,), (0,))).astype(BF16)
    query_self = proj[..., :cols]
    keys_self = proj[..., cols : cols + kv_half]
    values_self = proj[..., cols + kv_half :]
    mixed_self, log_self = attend_forward(query_self, keys_self, values_self, bias, causal)
    o1 = jnp.concatenate(exchange(pieces_of(mixed_self)), axis=-1)
    x0 = piece(start, 0)
    x1 = x0 + mm(o1, w_so, ((1,), (1,)))
    n2 = rms_norm(x1, gains[1]).astype(BF16)
    q2 = mm(n2, w_cq, ((1,), (0,))).astype(BF16)
    own_memory = lax.dynamic_index_in_dim(memory, t // split, 0, False)
    kv2 = mm(own_memory, w_ckv, ((1,), (0,))).astype(BF16)
    span = kv2.shape[0]
    kv2 = kv2.reshape(span, tp_size, 2, kv_half)
    k2 = kv2[:, :, 0].reshape(1, span, -1)
    v2 = kv2[:, :, 1].reshape(1, span, -1)
    o2, log_cross = attend_forward(q2[None], k2, v2, None, None)
    x2 = x1 + mm(o2[0], w_co, ((1,), (1,)))
    n3 = rms_norm(x2, gains[2]).astype(BF16)
    n3_all = jnp.stack(spread(n3)).reshape(-1, width)
    ff2 = gate_up.shape[2] * 2
    hid = gate_up.shape[2]
    w_gu = w_ffn[:, :ff2]
    w_dn = w_ffn[:, ff2:]
    joined = mm(n3_all, w_gu, ((1,), (0,)))
    gate = joined[:, :hid]
    up = joined[:, hid:]
    hidden = gelu_product(gate, up).astype(BF16)
    out_part = mm(hidden, w_dn, ((1,), (1,))).astype(BF16).reshape(tp_size, chunk, width)
    cot = relative(cotangent.reshape(tp_size, chunk, width), t, tp_size)
    y3 = cot.reshape(-1, width)
    grad_hidden = mm(y3, w_dn, ((1,), (0,)))
    _, pull = jax.vjp(gelu_product, gate, up)
    grad_gate, grad_up = pull(grad_hidden)
    grad_joined = jnp.concatenate([grad_gate, grad_up], axis=-1).astype(BF16)
    dn3_part = mm(grad_joined, w_gu, ((1,), (1,))).astype(BF16).reshape(tp_size, chunk, width)

    def total(pieces):
        acc = pieces[0].astype(F32)
        for p in pieces[1:]:
            acc = acc + p.astype(F32)
        return acc

    dn3 = total(exchange([dn3_part[j] for j in range(tp_size)]))
    out = x2 + total(exchange([out_part[j] for j in range(tp_size)]))
    decoder_out = placed(spread(out.astype(BF16))).reshape(decoder_in.shape)
    gu_grad = mm(n3_all, grad_joined, ((0,), (0,))).astype(BF16)
    dn_grad = mm(y3, hidden, ((0,), (0,))).astype(BF16)
    ffn_grad = lax.psum_scatter(
        jnp.concatenate([gu_grad, dn_grad], axis=1), zf, scatter_dimension=0, tiled=True
    )
    e3 = cot[0].astype(F32)
    _, pull = jax.vjp(rms_norm, x2, gains[2])
    dv, dg2 = pull(dn3)
    e2 = e3 + dv
    y2 = e2.astype(BF16)
    do2 = mm(y2, w_co, ((1,), (0,))).astype(BF16)
    dq2, dk2, dv2, _ = attend_backward(q2[None], k2, v2, None, None, log_cross, do2[None])
    dq2 = dq2[0]
    dkv2 = jnp.stack(
        [dk2[0].reshape(span, tp_size, kv_half), dv2[0].reshape(span, tp_size, kv_half)], axis=2
    ).reshape(span, -1)
    dn2 = mm(dq2, w_cq, ((1,), (1,)))
    _, pull = jax.vjp(rms_norm, x1, gains[1])
    dv, dg1 = pull(dn2)
    e1 = e2 + dv
    y1 = e1.astype(BF16)
    do1_full = mm(y1, w_so, ((1,), (0,))).astype(BF16)
    do1 = whole_rows(exchange([do1_full[:, j * cols : (j + 1) * cols] for j in range(tp_size)]))
    quarter = width // tp_size
    w_rows = w_ckv.reshape(tp_size, quarter, -1)
    mem_pieces = []
    for j in range(tp_size):
        w_j = lax.dynamic_index_in_dim(w_rows, t ^ j, 0, False)
        mem_pieces.append(mm(dkv2, w_j, ((1,), (1,))).astype(BF16))
    mem_got = exchange(mem_pieces)
    memory_grad = jnp.zeros((batch,) + mem_got[0].shape, BF16)
    for b in range(batch):
        own = mem_got[b * split]
        if split > 1:
            own = total(mem_got[b * split : (b + 1) * split]).astype(BF16)
        memory_grad = lax.dynamic_update_index_in_dim(memory_grad, own, t // split ^ b, 0)

    def core_sum(grad):
        g = grad.reshape(seq_size, 2, shard, -1)
        mine = lax.dynamic_index_in_dim(g, f, 1, False)
        theirs = lax.dynamic_index_in_dim(g, 1 - f, 1, False)
        return (mine.astype(F32) + swap_core(theirs).astype(F32)).astype(BF16)

    def tp_sum(parts):
        pieces = [
            jnp.concatenate([p[..., j * cols : (j + 1) * cols] for p in parts], axis=-1)
            for j in range(tp_size)
        ]
        return total(exchange(pieces)).astype(BF16)

    g_co = core_sum(mm(y2, o2[0], ((0,), (0,))).astype(BF16))
    g_cq = core_sum(mm(n2, dq2, ((0,), (0,))).astype(BF16))
    g_ckv = core_sum(mm(own_memory, dkv2, ((0,), (0,))).astype(BF16))
    g_so = core_sum(mm(y1, o1, ((0,), (0,))).astype(BF16))
    full_grad = tp_sum([g_co, g_cq, g_ckv, g_so])
    full_grad = lax.psum_scatter(full_grad, "seq", scatter_dimension=0, tiled=False)
    dq1, dk1, dv1, ds1 = attend_backward(
        query_self, keys_self, values_self, bias, causal, log_self, do1
    )
    table_grad = jnp.einsum(
        "ijn,bhij->nh", onehot, ds1.reshape(batch, -1, rows, rows), preferred_element_type=F32
    )
    dproj = jnp.concatenate([dq1, dk1, dv1], axis=-1)
    dn1_part = mm(dproj, w_self, ((2,), (1,))).astype(BF16)
    self_grad = lax.psum_scatter(
        mm(normed_self.reshape(-1, width), dproj.reshape(-1, dproj.shape[-1]), ((0,), (0,))).astype(
            BF16
        ),
        zf,
        scatter_dimension=0,
        tiled=True,
    )
    dn1 = total(exchange(pieces_of(dn1_part)))
    _, pull = jax.vjp(rms_norm, x0, gains[0])
    dv, dg0 = pull(dn1)
    decoder_grad = placed(spread((e1 + dv).astype(BF16))).reshape(decoder_in.shape).astype(F32)
    small = jnp.stack([dg0, dg1, dg2, jnp.pad(table_grad.reshape(-1), (0, width - NB * heads))])
    small = lax.all_gather(small, ("seq", "fsdp", "tp"), axis=0, tiled=False)
    place = s * 2 + f
    gains_grad = lax.dynamic_slice_in_dim(jnp.sum(small[:, :3], axis=0), place * shard, shard, 1)
    tables = small[:, 3, : NB * heads].reshape(-1, tp_size, NB * heads)
    tables = jnp.sum(lax.dynamic_index_in_dim(tables, t, 1, False), axis=0).reshape(NB, heads)
    bias_grad = lax.dynamic_slice_in_dim(tables, place * tb_rows, tb_rows, 0)
    full_grad = full_grad.astype(F32)
    self_grad = self_grad.astype(F32)
    ffn_grad = ffn_grad.astype(F32)
    return (
        decoder_out,
        decoder_grad,
        memory_grad,
        gains_grad,
        bias_grad,
        self_grad[:, :cols],
        self_grad[:, cols:].reshape(self_kv.shape),
        full_grad[:, 3 * cols :].T,
        full_grad[:, cols : 2 * cols],
        full_grad[:, 2 * cols : 3 * cols].reshape(cross_kv.shape),
        full_grad[:, :cols].T,
        ffn_grad[:, :ff2].reshape(gate_up.shape),
        ffn_grad[:, ff2:].T,
    )


def solution(mesh):
    tp_size = mesh.shape["tp"]
    seq_size = mesh.shape["seq"]

    def body(*args):
        return per_device(*args, tp_size=tp_size, seq_size=seq_size)

    both = ("seq", "fsdp")
    token = P(both, None, None)
    weight = P(both, "tp")
    paired = P(both, None, "tp")
    turned = P("tp", both)
    return jax.shard_map(
        body,
        mesh=mesh,
        in_specs=(
            token,
            token,
            P(),
            P(None, both),
            weight,
            weight,
            paired,
            turned,
            weight,
            paired,
            turned,
            paired,
            turned,
            token,
        ),
        out_specs=(
            token,
            token,
            P(both, None, "tp"),
            P(None, both),
            weight,
            weight,
            paired,
            turned,
            weight,
            paired,
            turned,
            paired,
            turned,
        ),
        check_vma=False,
    )
```

profile of v0, /device:TPU:0, one launch (start us, length us, event | category | flops | bytes accessed | tf_op | source)
XLA Modules:
  0.0 551.6 jit_solution(9025525953042338345)
XLA Ops:
  15.4 13.5 %all_gather.28 = bf16[8,4,128]{2,1,0:T(4,128)(2,1)S(1)} all-gather(bf16[1,4,128]{2,1,0:T(4,128)(2,1)S(1)} %scatter.9), channel_id=1, replica_groups=mesh['seq'=4,'tp'=4,'fsdp'=2] {'seq','fsdp'}, dimensions={0}, use_global_device_ids=true | all-gather | bytes 9216 | tf_op jit(solution)/shard_map/all_gather | solution.py:167
  34.0 8.6 %all-gather.11.cloned.1.call-done = bf16[8,128,512]{2,1,0:T(8,128)(2,1)} async-done(((bf16[2,128,512]{2,1,0:T(8,128)(2,1)}), bf16[8,128,512]{2,1,0:T(8,128)(2,1)}) %all-gather.11.cloned.1.call-update) | async-done | bytes 1048592 | tf_op jit(solution)/shard_map/all_gather | solution.py:176
  44.9 2.4 collective-permute-start.8
  48.9 17.2 %all-gather.7.cloned.1.call-done = bf16[1024,512]{1,0:T(8,128)(2,1)} async-done(((bf16[128,512]{1,0:T(8,128)(2,1)}), bf16[1024,512]{1,0:T(8,128)(2,1)}) %all-gather.7.cloned.1.call-update) | async-done | bytes 1048592 | tf_op jit(solution)/shard_map/all_gather | solution.py:178
  74.6 2.4 collective-permute-start.15
  83.1 2.3 collective-permute-start.2
  86.5 4.1 collective-permute-done.15
  93.7 8.1 %collective-permute-done.13 = bf16[4,128,512]{2,1,0:T(8,128)(2,1)S(1)} collective-permute-done((bf16[4,128,512]{2,1,0:T(8,128)(2,1)}, bf16[4,128,512]{2,1,0:T(8,128)(2,1)S(1)}, u32[]{:S(2)}, u32[]{:S(2)}) %collective-permute-start.13) | collective-permute-done | bytes 524320 | tf_op jit(solution)/shard_map/ppermute | solution.py:117
  112.4 7.5 %fusion.21 = bf16[2048,1024]{0,1:T(8,128)(2,1)S(1)} fusion(bf16[4,2048,1024]{2,1,0:T(8,128)(2,1)} %param.19, s32[]{:T(128)S(6)} %select_n.140, bf16[1024,256]{1,0:T(8,128)(2,1)S(1)} %get-tuple-element.184, bf16[1024,256]{1,0:T(8,128)(2,1)S(1)} %copy-done.39, bf16[1024,256]{1,0:T(8,128)(2,1)S(1)} %copy-done.40, bf16[1024,256]{1,0:T(8,128)(2,1)S(1)} %get-tuple-element.178), kind=kOutput, calls=%fused_computation.31 | convolution fusion | flops 4305453056 | bytes 10485764 | tf_op jit(solution)/shard_map/dot_general | solution.py:23
  120.3 8.2 %bitcast_reduce_fusion = (f32[8,2,128]{2,1,0:T(2,128)S(1)}, f32[8,2048,128,2]{2,1,3,0:T(8,128)}) fusion(bf16[2048,8,64,1]{0,2,3,1:T(8,128)(2,1)S(1)} %bitcast.415, bf16[128,8,2,64]{0,3,2,1:T(8,128)(2,1)S(1)} %bitcast.424), kind=kOutput, calls=%fused_computation.7 | convolution fusion | flops 545257472 | bytes 19144704 | tf_op jit(solution)/shard_map/bigrd,bjgd->bgrij/dot_general | solution.py:39
  128.5 8.6 %fusion.5 = f32[8,2,128]{2,1,0:T(2,128)S(1)} fusion(f32[8,2048,128,2]{2,1,3,0:T(8,128)} %get-tuple-element.220, f32[8,2,128]{2,1,0:T(2,128)S(1)} %get-tuple-element.219), kind=kLoop, calls=%fused_computation.11 | loop fusion | flops 12580864 | bytes 16793600 | tf_op jit(solution)/shard_map/reduce_sum | solution.py:54
  137.1 7.7 %fusion.63 = bf16[8,64,2,128]{3,1,2,0:T(8,128)(2,1)S(1)} fusion(bf16[2048,8,64,1]{0,2,3,1:T(8,128)(2,1)S(1)} %bitcast.421, f32[8,2,128]{2,1,0:T(2,128)S(1)} %fusion.5, f32[8,2,128]{2,1,0:T(2,128)S(1)} %get-tuple-element.219, f32[8,2048,128,2]{2,1,3,0:T(8,128)} %get-tuple-element.220), kind=kOutput, calls=%fused_computation.104 | convolution fusion | flops 553779200 | bytes 19152896 | tf_op jit(solution)/shard_map/bgrij,bjgd->bigrd/dot_general | solution.py:56
  151.5 5.4 collective-permute-done.19
  156.9 4.8 collective-permute-done.18
  163.8 4.1 fusion.30
  167.9 2.9 fusion.51
  176.4 6.6 %collective-permute-done.28 = bf16[128,1024]{1,0:T(8,128)(2,1)S(1)} collective-permute-done((bf16[128,1024]{1,0:T(8,128)(2,1)S(1)}, bf16[128,1024]{1,0:T(8,128)(2,1)S(1)}, u32[]{:S(2)}, u32[]{:S(2)}) %collective-permute-start.28) | collective-permute-done | bytes 262176 | tf_op jit(solution)/shard_map/ppermute | solution.py:117
  182.9 4.6 collective-permute-done.27
  191.6 11.9 %fusion = (f32[8,2,128]{2,1,0:T(2,128)S(1)}, f32[8,2048,128,2]{2,1,3,0:T(8,128)}) fusion(f32[8,2048,128,2]{2,1,3,0:T(8,128)} %get-tuple-element.220, f32[8,2,128]{2,1,0:T(2,128)S(1)} %bitcast.490, bf16[2048,8,64,1]{0,2,3,1:T(8,128)(2,1)} %bitcast.422, bf16[128,8,2,64]{0,3,2,1:T(8,128)(2,1)} %bitcast.442), kind=kOutput, calls=%fused_computation.2 | convolution fusion | flops 553646080 | bytes 35930112 | tf_op jit(solution)/shard_map/bigrd,bjgd->bgrij/dot_general | solution.py:64
  203.5 10.1 %bitcast_convert_fusion = bf16[8,64,2048]{2,1,0:T(8,128)(2,1)} fusion(bf16[128,8,2,64]{0,3,2,1:T(8,128)(2,1)S(1)} %bitcast.443, f32[8,2048,128,2]{2,1,3,0:T(8,128)} %get-tuple-element.220, f32[8,2,128]{2,1,0:T(2,128)S(1)} %bitcast.491), kind=kOutput, calls=%fused_computation.23 | convolution fusion | flops 550502400 | bytes 19144704 | tf_op jit(solution)/shard_map/bgrij,bigrd->bjgd/dot_general | solution.py:77
  213.6 12.0 %fusion.10 = bf16[8,2,128,2048]{2,3,1,0:T(8,128)(2,1)S(1)} fusion(f32[8,2048,128,2]{2,1,3,0:T(8,128)} %get-tuple-element.224, f32[8,2048,128,2]{2,1,3,0:T(8,128)} %get-tuple-element.220, f32[8,2,128]{2,1,0:T(2,128)S(1)} %get-tuple-element.223, f32[8,2,128]{2,1,0:T(2,128)S(1)} %bitcast.492), kind=kLoop, calls=%fused_computation.15 | loop fusion | flops 20971520 | bytes 41959424 | tf_op jit(solution)/shard_map/reshape.150
  227.2 2.7 fusion.16
  243.8 2.3 copy.276
  248.1 8.6 %fusion.42 = bf16[1024,1024]{1,0:T(8,128)(2,1)S(1)} fusion(bf16[2048,1024]{0,1:T(8,128)(2,1)S(1)} %bitcast.428, bf16[4,2048,1024]{2,1,0:T(8,128)(2,1)} %param.19, s32[]{:T(128)S(6)} %select_n.140), kind=kOutput, calls=%fused_computation.66 | convolution fusion | flops 4296015872 | bytes 10485764 | tf_op jit(solution)/shard_map/dot_general | solution.py:23
  258.3 2.5 copy.274
  271.7 2.4 copy.270
  284.3 3.0 bitcast_convert_fusion.1
  297.9 23.2 %collective-permute-done.47 = bf16[4,128,1024]{1,2,0:T(8,128)(2,1)S(1)} collective-permute-done((bf16[4,128,1024]{1,2,0:T(8,128)(2,1)S(1)}, bf16[4,128,1024]{1,2,0:T(8,128)(2,1)S(1)}, u32[]{:S(2)}, u32[]{:S(2)}) %collective-permute-start.47) | collective-permute-done | bytes 1048608 | tf_op jit(solution)/shard_map/ppermute | solution.py:117
  321.1 21.5 %collective-permute-done.46 = bf16[4,128,1024]{1,2,0:T(8,128)(2,1)S(1)} collective-permute-done((bf16[4,128,1024]{1,2,0:T(8,128)(2,1)S(1)}, bf16[4,128,1024]{1,2,0:T(8,128)(2,1)S(1)}, u32[]{:S(2)}, u32[]{:S(2)}) %collective-permute-start.46) | collective-permute-done | bytes 1048608 | tf_op jit(solution)/shard_map/ppermute | solution.py:117
  344.2 3.5 convolution_convert_fusion.8
  349.4 3.5 convolution_convert_fusion
  353.0 2.4 pad_maximum_fusion
  357.1 2.6 convolution_convert_fusion.9
  367.1 4.9 collective-permute-done.22
  371.9 4.7 collective-permute-done.21
  382.8 2.3 convolution_convert_fusion.3
  385.7 2.3 convolution_convert_fusion.2
  388.0 2.4 convolution_convert_fusion.1
  390.5 2.3 broadcast_in_dim.90
  392.8 2.3 fusion.33
  410.6 11.7 %collective-permute-done.34 = bf16[128,1024]{1,0:T(8,128)(2,1)S(1)} collective-permute-done((bf16[128,1024]{1,0:T(8,128)(2,1)}, bf16[128,1024]{1,0:T(8,128)(2,1)S(1)}, u32[]{:S(2)}, u32[]{:S(2)}) %collective-permute-start.34) | collective-permute-done | bytes 262176 | tf_op jit(solution)/shard_map/ppermute | solution.py:117
  423.8 4.1 collective-permute-done.32
  433.5 83.1 %all-gather.2 = f32[32,4,1024]{2,1,0:T(4,128)S(1)} all-gather(f32[1,4,1024]{2,1,0:T(4,128)S(1)} %maximum_bitcast_fusion.2), channel_id=3, replica_groups=mesh['seq'=4,'tp'=4,'fsdp'=2] {'seq','fsdp','tp'}, dimensions={0}, use_global_device_ids=true | all-gather | bytes 540672 | tf_op jit(solution)/shard_map/all_gather | solution.py:328
  519.4 5.8 %collective-permute-done.37 = bf16[128,1024]{1,0:T(8,128)(2,1)S(1)} collective-permute-done((bf16[128,1024]{1,0:T(8,128)(2,1)S(1)}, bf16[128,1024]{1,0:T(8,128)(2,1)S(1)}, u32[]{:S(2)}, u32[]{:S(2)}) %collective-permute-start.37) | collective-permute-done | bytes 262176 | tf_op jit(solution)/shard_map/ppermute | solution.py:117
  526.0 2.8 convert_element_type.361
  528.8 2.3 bitcast_dynamic-update-slice_fusion.2
  531.0 2.3 bitcast_dynamic-update-slice_fusion.1
  533.3 2.3 bitcast_dynamic-update-slice_fusion
  (478 shorter events, 168.5 us)
Async XLA Ops:
  7.2 35.4 %all-gather.11.cloned.1.call-start = ((), (), s32[]{:S(2)}) async-start(), calls=%async_computation.8 | async-start | bytes 1310720 | tf_op jit(solution)/shard_map/all_gather | solution.py:176
  11.7 54.3 %all-gather.7.cloned.1.call-start = ((), (), s32[]{:S(2)}) async-start(), calls=%async_computation.3 | async-start | bytes 1179648 | tf_op jit(solution)/shard_map/all_gather | solution.py:178
  14.2 149.6 %all-gather.9.cloned.1.call-start = ((), (), s32[]{:S(2)}) async-start(), calls=%async_computation.4 | async-start | bytes 4866048 | tf_op jit(solution)/shard_map/all_gather | solution.py:180
  15.1 520.5 %reduce-scatter.4.cloned.1.call-start = ((), (), s32[]{:S(2)}) async-start(), calls=%async_computation.5 | async-start | bytes 1179648 | tf_op jit(solution)/shard_map/reduce_scatter | solution.py:315
  44.9 34.6 %collective-permute-start.8 = (bf16[4,128,512]{2,1,0:T(8,128)(2,1)}, bf16[4,128,512]{2,1,0:T(8,128)(2,1)}, u32[]{:S(2)}, u32[]{:S(2)}) collective-permute-start(bf16[4,128,512]{2,1,0:T(8,128)(2,1)} %get-tuple-element.177), channel_id=1, source_target_pairs={{0,6},{2,4},{4,2},{6,0},{1,7},{3,5},{5,3},{7,1},{8,14},{10,12},{12... | collective-permute-start | bytes 1572872 | tf_op jit(solution)/shard_map/ppermute | solution.py:117
  47.3 32.3 %collective-permute-start.6 = (bf16[4,128,512]{2,1,0:T(8,128)(2,1)}, bf16[4,128,512]{2,1,0:T(8,128)(2,1)}, u32[]{:S(2)}, u32[]{:S(2)}) collective-permute-start(bf16[4,128,512]{2,1,0:T(8,128)(2,1)} %get-tuple-element.177), channel_id=1, source_target_pairs={{0,4},{2,6},{4,0},{6,2},{1,5},{3,7},{5,1},{7,3},{8,12},{10,14},{12... | collective-permute-start | bytes 1572872 | tf_op jit(solution)/shard_map/ppermute | solution.py:117
  47.8 33.3 %collective-permute-start.4 = (bf16[4,128,512]{2,1,0:T(8,128)(2,1)}, bf16[4,128,512]{2,1,0:T(8,128)(2,1)}, u32[]{:S(2)}, u32[]{:S(2)}) collective-permute-start(bf16[4,128,512]{2,1,0:T(8,128)(2,1)} %get-tuple-element.177), channel_id=1, source_target_pairs={{0,2},{2,0},{4,6},{6,4},{1,3},{3,1},{5,7},{7,5},{8,10},{10,8},{12,... | collective-permute-start | bytes 1572872 | tf_op jit(solution)/shard_map/ppermute | solution.py:117
  48.4 28.7 %collective-permute-start.3 = (bf16[4,128,512]{2,1,0:T(8,128)(2,1)}, bf16[4,128,512]{2,1,0:T(8,128)(2,1)}, u32[]{:S(2)}, u32[]{:S(2)}) collective-permute-start(bf16[4,128,512]{2,1,0:T(8,128)(2,1)} %get-tuple-element.177), channel_id=1, source_target_pairs={{0,1},{1,0},{2,3},{3,2},{4,5},{5,4},{6,7},{7,6},{8,9},{9,8},{10,11... | collective-permute-start | bytes 1572872 | tf_op jit(solution)/shard_map/ppermute | solution.py:120
  48.4 26.2 %collective-permute-start.10 = (bf16[4,128,512]{2,1,0:T(8,128)(2,1)}, bf16[4,128,512]{2,1,0:T(8,128)(2,1)}, u32[]{:S(2)}, u32[]{:S(2)}) collective-permute-start(bf16[4,128,512]{2,1,0:T(8,128)(2,1)} %get-tuple-element.176), channel_id=1, source_target_pairs={{0,1},{1,0},{2,3},{3,2},{4,5},{5,4},{6,7},{7,6},{8,9},{9,8},{10,11... | collective-permute-start | bytes 1572872 | tf_op jit(solution)/shard_map/ppermute | solution.py:120
  74.6 16.0 %collective-permute-start.15 = (bf16[4,128,512]{2,1,0:T(8,128)(2,1)}, bf16[4,128,512]{2,1,0:T(8,128)(2,1)S(1)}, u32[]{:S(2)}, u32[]{:S(2)}) collective-permute-start(bf16[4,128,512]{2,1,0:T(8,128)(2,1)} %get-tuple-element.176), channel_id=1, source_target_pairs={{0,6},{2,4},{4,2},{6,0},{1,7},{3,5},{5,3},{7,1},{8,14},{10,12},{12... | collective-permute-start | bytes 1572872 | tf_op jit(solution)/shard_map/ppermute | solution.py:117
  77.0 24.8 %collective-permute-start.13 = (bf16[4,128,512]{2,1,0:T(8,128)(2,1)}, bf16[4,128,512]{2,1,0:T(8,128)(2,1)S(1)}, u32[]{:S(2)}, u32[]{:S(2)}) collective-permute-start(bf16[4,128,512]{2,1,0:T(8,128)(2,1)} %get-tuple-element.176), channel_id=1, source_target_pairs={{0,4},{2,6},{4,0},{6,2},{1,5},{3,7},{5,1},{7,3},{8,12},{10,14},{12... | collective-permute-start | bytes 1572872 | tf_op jit(solution)/shard_map/ppermute | solution.py:117
  81.1 22.3 %collective-permute-start.11 = (bf16[4,128,512]{2,1,0:T(8,128)(2,1)}, bf16[4,128,512]{2,1,0:T(8,128)(2,1)S(1)}, u32[]{:S(2)}, u32[]{:S(2)}) collective-permute-start(bf16[4,128,512]{2,1,0:T(8,128)(2,1)} %get-tuple-element.176), channel_id=1, source_target_pairs={{0,2},{2,0},{4,6},{6,4},{1,3},{3,1},{5,7},{7,5},{8,10},{10,8},{12,... | collective-permute-start | bytes 1572872 | tf_op jit(solution)/shard_map/ppermute | solution.py:117
  81.7 10.4 %collective-permute-start.5 = (bf16[4,128,512]{2,1,0:T(8,128)(2,1)}, bf16[4,128,512]{2,1,0:T(8,128)(2,1)S(1)}, u32[]{:S(2)}, u32[]{:S(2)}) collective-permute-start(bf16[4,128,512]{2,1,0:T(8,128)(2,1)} %collective-permute-done.4), channel_id=1, source_target_pairs={{0,1},{1,0},{2,3},{3,2},{4,5},{5,4},{6,7},{7,6},{8,9},{9,8},{10,11... | collective-permute-start | bytes 1572872 | tf_op jit(solution)/shard_map/ppermute | solution.py:120
  83.1 26.2 %collective-permute-start.2 = (bf16[128,256]{0,1:T(8,128)(2,1)S(1)}, bf16[128,256]{0,1:T(8,128)(2,1)S(1)}, u32[]{:S(2)}, u32[]{:S(2)}) collective-permute-start(bf16[128,256]{0,1:T(8,128)(2,1)S(1)} %bitcast.502), channel_id=1, source_target_pairs={{0,6},{2,4},{4,2},{6,0},{1,7},{3,5},{5,3},{7,1},{8,14},{10,12},{12... | collective-permute-start | bytes 196616 | tf_op jit(solution)/shard_map/ppermute | solution.py:117
  90.6 18.7 %collective-permute-start.1 = (bf16[128,256]{0,1:T(8,128)(2,1)S(1)}, bf16[128,256]{0,1:T(8,128)(2,1)S(1)}, u32[]{:S(2)}, u32[]{:S(2)}) collective-permute-start(bf16[128,256]{0,1:T(8,128)(2,1)S(1)} %bitcast.501), channel_id=1, source_target_pairs={{0,4},{2,6},{4,0},{6,2},{1,5},{3,7},{5,1},{7,3},{8,12},{10,14},{12... | collective-permute-start | bytes 196616 | tf_op jit(solution)/shard_map/ppermute | solution.py:117
  92.1 11.3 %collective-permute-start.16 = (bf16[4,128,512]{2,1,0:T(8,128)(2,1)S(1)}, bf16[4,128,512]{2,1,0:T(8,128)(2,1)S(1)}, u32[]{:S(2)}, u32[]{:S(2)}) collective-permute-start(bf16[4,128,512]{2,1,0:T(8,128)(2,1)S(1)} %collective-permute-done.15), channel_id=1, source_target_pairs={{0,1},{1,0},{2,3},{3,2},{4,5},{5,4},{6,7},{7,6},{8,9},{9,8},{10,11... | collective-permute-start | bytes 1572872 | tf_op jit(solution)/shard_map/ppermute | solution.py:120
  146.7 10.2 %collective-permute-start.19 = (bf16[128,1024]{1,0:T(8,128)(2,1)S(1)}, bf16[128,1024]{1,0:T(8,128)(2,1)S(1)}, u32[]{:S(2)}, u32[]{:S(2)}) collective-permute-start(bf16[128,1024]{1,0:T(8,128)(2,1)S(1)} %multiply_convert_fusion.4), channel_id=1, source_target_pairs={{0,6},{2,4},{4,2},{6,0},{1,7},{3,5},{5,3},{7,1},{8,14},{10,12},{12... | collective-permute-start | bytes 786440 | tf_op jit(solution)/shard_map/ppermute | solution.py:117
  148.3 13.4 %collective-permute-start.18 = (bf16[128,1024]{1,0:T(8,128)(2,1)S(1)}, bf16[128,1024]{1,0:T(8,128)(2,1)}, u32[]{:S(2)}, u32[]{:S(2)}) collective-permute-start(bf16[128,1024]{1,0:T(8,128)(2,1)S(1)} %multiply_convert_fusion.4), channel_id=1, source_target_pairs={{0,4},{2,6},{4,0},{6,2},{1,5},{3,7},{5,1},{7,3},{8,12},{10,14},{12... | collective-permute-start | bytes 786440 | tf_op jit(solution)/shard_map/ppermute | solution.py:117
  148.8 12.8 %collective-permute-start.17 = (bf16[128,1024]{1,0:T(8,128)(2,1)S(1)}, bf16[128,1024]{1,0:T(8,128)(2,1)}, u32[]{:S(2)}, u32[]{:S(2)}) collective-permute-start(bf16[128,1024]{1,0:T(8,128)(2,1)S(1)} %multiply_convert_fusion.4), channel_id=1, source_target_pairs={{0,2},{2,0},{4,6},{6,4},{1,3},{3,1},{5,7},{7,5},{8,10},{10,8},{12,... | collective-permute-start | bytes 786440 | tf_op jit(solution)/shard_map/ppermute | solution.py:117
  172.8 10.2 %collective-permute-start.28 = (bf16[128,1024]{1,0:T(8,128)(2,1)S(1)}, bf16[128,1024]{1,0:T(8,128)(2,1)S(1)}, u32[]{:S(2)}, u32[]{:S(2)}) collective-permute-start(bf16[128,1024]{1,0:T(8,128)(2,1)S(1)} %get-tuple-element.151), channel_id=1, source_target_pairs={{0,6},{2,4},{4,2},{6,0},{1,7},{3,5},{5,3},{7,1},{8,14},{10,12},{12... | collective-permute-start | bytes 786440 | tf_op jit(solution)/shard_map/ppermute | solution.py:117
  174.3 13.3 %collective-permute-start.27 = (bf16[128,1024]{1,0:T(8,128)(2,1)S(1)}, bf16[128,1024]{1,0:T(8,128)(2,1)S(1)}, u32[]{:S(2)}, u32[]{:S(2)}) collective-permute-start(bf16[128,1024]{1,0:T(8,128)(2,1)S(1)} %get-tuple-element.152), channel_id=1, source_target_pairs={{0,4},{2,6},{4,0},{6,2},{1,5},{3,7},{5,1},{7,3},{8,12},{10,14},{12... | collective-permute-start | bytes 786440 | tf_op jit(solution)/shard_map/ppermute | solution.py:117
  174.9 12.7 %collective-permute-start.26 = (bf16[128,1024]{1,0:T(8,128)(2,1)S(1)}, bf16[128,1024]{1,0:T(8,128)(2,1)S(1)}, u32[]{:S(2)}, u32[]{:S(2)}) collective-permute-start(bf16[128,1024]{1,0:T(8,128)(2,1)S(1)} %get-tuple-element.150), channel_id=1, source_target_pairs={{0,2},{2,0},{4,6},{6,4},{1,3},{3,1},{5,7},{7,5},{8,10},{10,8},{12,... | collective-permute-start | bytes 786440 | tf_op jit(solution)/shard_map/ppermute | solution.py:117
  238.0 37.4 %collective-permute-start.31 = (bf16[128,256]{1,0:T(8,128)(2,1)}, bf16[128,256]{1,0:T(8,128)(2,1)}, u32[]{:S(2)}, u32[]{:S(2)}) collective-permute-start(bf16[128,256]{1,0:T(8,128)(2,1)} %get-tuple-element.203), channel_id=1, source_target_pairs={{0,6},{2,4},{4,2},{6,0},{1,7},{3,5},{5,3},{7,1},{8,14},{10,12},{12... | collective-permute-start | bytes 196616 | tf_op jit(solution)/shard_map/ppermute | solution.py:117
  239.5 36.9 %collective-permute-start.30 = (bf16[128,256]{1,0:T(8,128)(2,1)}, bf16[128,256]{1,0:T(8,128)(2,1)}, u32[]{:S(2)}, u32[]{:S(2)}) collective-permute-start(bf16[128,256]{1,0:T(8,128)(2,1)} %get-tuple-element.204), channel_id=1, source_target_pairs={{0,4},{2,6},{4,0},{6,2},{1,5},{3,7},{5,1},{7,3},{8,12},{10,14},{12... | collective-permute-start | bytes 196616 | tf_op jit(solution)/shard_map/ppermute | solution.py:117
  240.1 37.8 %collective-permute-start.29 = (bf16[128,256]{1,0:T(8,128)(2,1)}, bf16[128,256]{1,0:T(8,128)(2,1)S(1)}, u32[]{:S(2)}, u32[]{:S(2)}) collective-permute-start(bf16[128,256]{1,0:T(8,128)(2,1)} %get-tuple-element.205), channel_id=1, source_target_pairs={{0,2},{2,0},{4,6},{6,4},{1,3},{3,1},{5,7},{7,5},{8,10},{10,8},{12,... | collective-permute-start | bytes 196616 | tf_op jit(solution)/shard_map/ppermute | solution.py:117
  246.1 41.3 %collective-permute-start.44 = (bf16[4,128,1024]{1,2,0:T(8,128)(2,1)}, bf16[4,128,1024]{1,2,0:T(8,128)(2,1)}, u32[]{:S(2)}, u32[]{:S(2)}) collective-permute-start(bf16[4,128,1024]{1,2,0:T(8,128)(2,1)} %bitcast.458), channel_id=1, source_target_pairs={{0,1},{1,0},{2,3},{3,2},{4,5},{5,4},{6,7},{7,6},{8,9},{9,8},{10,11... | collective-permute-start | bytes 3145736 | tf_op jit(solution)/shard_map/ppermute | solution.py:120
  260.8 28.3 %collective-permute-start.43 = (bf16[4,128,1024]{1,2,0:T(8,128)(2,1)}, bf16[4,128,1024]{1,2,0:T(8,128)(2,1)}, u32[]{:S(2)}, u32[]{:S(2)}) collective-permute-start(bf16[4,128,1024]{1,2,0:T(8,128)(2,1)} %bitcast.459), channel_id=1, source_target_pairs={{0,1},{1,0},{2,3},{3,2},{4,5},{5,4},{6,7},{7,6},{8,9},{9,8},{10,11... | collective-permute-start | bytes 3145736 | tf_op jit(solution)/shard_map/ppermute | solution.py:120
  275.4 15.3 %collective-permute-start.42 = (bf16[4,128,1024]{1,2,0:T(8,128)(2,1)}, bf16[4,128,1024]{1,2,0:T(8,128)(2,1)}, u32[]{:S(2)}, u32[]{:S(2)}) collective-permute-start(bf16[4,128,1024]{1,2,0:T(8,128)(2,1)} %bitcast.461), channel_id=1, source_target_pairs={{0,1},{1,0},{2,3},{3,2},{4,5},{5,4},{6,7},{7,6},{8,9},{9,8},{10,11... | collective-permute-start | bytes 3145736 | tf_op jit(solution)/shard_map/ppermute | solution.py:120
  276.4 15.9 %collective-permute-start.41 = (bf16[4,128,1024]{1,2,0:T(8,128)(2,1)}, bf16[4,128,1024]{1,2,0:T(8,128)(2,1)}, u32[]{:S(2)}, u32[]{:S(2)}) collective-permute-start(bf16[4,128,1024]{1,2,0:T(8,128)(2,1)} %bitcast.460), channel_id=1, source_target_pairs={{0,1},{1,0},{2,3},{3,2},{4,5},{5,4},{6,7},{7,6},{8,9},{9,8},{10,11... | collective-permute-start | bytes 3145736 | tf_op jit(solution)/shard_map/ppermute | solution.py:120
  287.3 250.5 %reduce-scatter.6.cloned.1.call-start = ((), (), s32[]{:S(2)}) async-start(), calls=%async_computation.6 | async-start | bytes 1310720 | tf_op jit(solution)/shard_map/reduce_scatter | solution.py:306
  294.1 27.0 %collective-permute-start.47 = (bf16[4,128,1024]{1,2,0:T(8,128)(2,1)S(1)}, bf16[4,128,1024]{1,2,0:T(8,128)(2,1)S(1)}, u32[]{:S(2)}, u32[]{:S(2)}) collective-permute-start(bf16[4,128,1024]{1,2,0:T(8,128)(2,1)S(1)} %pad_maximum_fusion.19), channel_id=1, source_target_pairs={{0,6},{2,4},{4,2},{6,0},{1,7},{3,5},{5,3},{7,1},{8,14},{10,12},{12... | collective-permute-start | bytes 3145736 | tf_op jit(solution)/shard_map/ppermute | solution.py:117
  295.7 46.9 %collective-permute-start.46 = (bf16[4,128,1024]{1,2,0:T(8,128)(2,1)S(1)}, bf16[4,128,1024]{1,2,0:T(8,128)(2,1)S(1)}, u32[]{:S(2)}, u32[]{:S(2)}) collective-permute-start(bf16[4,128,1024]{1,2,0:T(8,128)(2,1)S(1)} %pad_maximum_fusion.18), channel_id=1, source_target_pairs={{0,4},{2,6},{4,0},{6,2},{1,5},{3,7},{5,1},{7,3},{8,12},{10,14},{12... | collective-permute-start | bytes 3145736 | tf_op jit(solution)/shard_map/ppermute | solution.py:117
  296.4 46.2 %collective-permute-start.45 = (bf16[4,128,1024]{1,2,0:T(8,128)(2,1)S(1)}, bf16[4,128,1024]{1,2,0:T(8,128)(2,1)S(1)}, u32[]{:S(2)}, u32[]{:S(2)}) collective-permute-start(bf16[4,128,1024]{1,2,0:T(8,128)(2,1)S(1)} %pad_maximum_fusion.17), channel_id=1, source_target_pairs={{0,2},{2,0},{4,6},{6,4},{1,3},{3,1},{5,7},{7,5},{8,10},{10,8},{12,... | collective-permute-start | bytes 3145736 | tf_op jit(solution)/shard_map/ppermute | solution.py:117
  344.2 196.9 %reduce-scatter.8.cloned.1.call-start = ((), (), s32[]{:S(2)}) async-start(), calls=%async_computation.7 | async-start | bytes 5013504 | tf_op jit(solution)/shard_map/reduce_scatter | solution.py:253
  361.6 10.3 %collective-permute-start.22 = (bf16[128,1024]{1,0:T(8,128)(2,1)}, bf16[128,1024]{1,0:T(8,128)(2,1)S(1)}, u32[]{:S(2)}, u32[]{:S(2)}) collective-permute-start(bf16[128,1024]{1,0:T(8,128)(2,1)} %get-tuple-element.158), channel_id=1, source_target_pairs={{0,6},{2,4},{4,2},{6,0},{1,7},{3,5},{5,3},{7,1},{8,14},{10,12},{12... | collective-permute-start | bytes 786440 | tf_op jit(solution)/shard_map/ppermute | solution.py:117
  363.2 13.4 %collective-permute-start.21 = (bf16[128,1024]{1,0:T(8,128)(2,1)}, bf16[128,1024]{1,0:T(8,128)(2,1)}, u32[]{:S(2)}, u32[]{:S(2)}) collective-permute-start(bf16[128,1024]{1,0:T(8,128)(2,1)} %get-tuple-element.159), channel_id=1, source_target_pairs={{0,4},{2,6},{4,0},{6,2},{1,5},{3,7},{5,1},{7,3},{8,12},{10,14},{12... | collective-permute-start | bytes 786440 | tf_op jit(solution)/shard_map/ppermute | solution.py:117
  363.8 12.8 %collective-permute-start.20 = (bf16[128,1024]{1,0:T(8,128)(2,1)}, bf16[128,1024]{1,0:T(8,128)(2,1)}, u32[]{:S(2)}, u32[]{:S(2)}) collective-permute-start(bf16[128,1024]{1,0:T(8,128)(2,1)} %get-tuple-element.157), channel_id=1, source_target_pairs={{0,2},{2,0},{4,6},{6,4},{1,3},{3,1},{5,7},{7,5},{8,10},{10,8},{12,... | collective-permute-start | bytes 786440 | tf_op jit(solution)/shard_map/ppermute | solution.py:117
  379.3 22.1 %collective-permute-start.23 = (bf16[128,1024]{1,0:T(8,128)(2,1)S(1)}, bf16[128,1024]{1,0:T(8,128)(2,1)S(1)}, u32[]{:S(2)}, u32[]{:S(2)}) collective-permute-start(bf16[128,1024]{1,0:T(8,128)(2,1)S(1)} %get-tuple-element.113), channel_id=1, source_target_pairs={{0,2},{2,0},{4,6},{6,4},{1,3},{3,1},{5,7},{7,5},{8,10},{10,8},{12,... | collective-permute-start | bytes 786440 | tf_op jit(solution)/shard_map/ppermute | solution.py:117
  379.9 25.3 %collective-permute-start.24 = (bf16[128,1024]{1,0:T(8,128)(2,1)S(1)}, bf16[128,1024]{1,0:T(8,128)(2,1)}, u32[]{:S(2)}, u32[]{:S(2)}) collective-permute-start(bf16[128,1024]{1,0:T(8,128)(2,1)S(1)} %get-tuple-element.113), channel_id=1, source_target_pairs={{0,4},{2,6},{4,0},{6,2},{1,5},{3,7},{5,1},{7,3},{8,12},{10,14},{12... | collective-permute-start | bytes 786440 | tf_op jit(solution)/shard_map/ppermute | solution.py:117
  381.3 26.2 %collective-permute-start.25 = (bf16[128,1024]{1,0:T(8,128)(2,1)S(1)}, bf16[128,1024]{1,0:T(8,128)(2,1)}, u32[]{:S(2)}, u32[]{:S(2)}) collective-permute-start(bf16[128,1024]{1,0:T(8,128)(2,1)S(1)} %get-tuple-element.113), channel_id=1, source_target_pairs={{0,6},{2,4},{4,2},{6,0},{1,7},{3,5},{5,3},{7,1},{8,14},{10,12},{12... | collective-permute-start | bytes 786440 | tf_op jit(solution)/shard_map/ppermute | solution.py:117
  385.1 143.7 %collective-permute-start.38 = (bf16[2048,256]{1,0:T(8,128)(2,1)}, bf16[2048,256]{1,0:T(8,128)(2,1)}, u32[]{:S(2)}, u32[]{:S(2)}) collective-permute-start(bf16[2048,256]{1,0:T(8,128)(2,1)} %convolution_convert_fusion.3), channel_id=1, source_target_pairs={{0,2},{2,0},{4,6},{6,4},{1,3},{3,1},{5,7},{7,5},{8,10},{10,8},{12,... | collective-permute-start | bytes 3145736 | tf_op jit(solution)/shard_map/ppermute | solution.py:117
  397.7 24.6 %collective-permute-start.34 = (bf16[128,1024]{1,0:T(8,128)(2,1)}, bf16[128,1024]{1,0:T(8,128)(2,1)S(1)}, u32[]{:S(2)}, u32[]{:S(2)}) collective-permute-start(bf16[128,1024]{1,0:T(8,128)(2,1)} %get-tuple-element.148), channel_id=1, source_target_pairs={{0,6},{2,4},{4,2},{6,0},{1,7},{3,5},{5,3},{7,1},{8,14},{10,12},{12... | collective-permute-start | bytes 786440 | tf_op jit(solution)/shard_map/ppermute | solution.py:117
  402.1 21.7 %collective-permute-start.33 = (bf16[128,1024]{1,0:T(8,128)(2,1)}, bf16[128,1024]{1,0:T(8,128)(2,1)S(1)}, u32[]{:S(2)}, u32[]{:S(2)}) collective-permute-start(bf16[128,1024]{1,0:T(8,128)(2,1)} %get-tuple-element.149), channel_id=1, source_target_pairs={{0,4},{2,6},{4,0},{6,2},{1,5},{3,7},{5,1},{7,3},{8,12},{10,14},{12... | collective-permute-start | bytes 786440 | tf_op jit(solution)/shard_map/ppermute | solution.py:117
  405.2 22.7 %collective-permute-start.32 = (bf16[128,1024]{1,0:T(8,128)(2,1)}, bf16[128,1024]{1,0:T(8,128)(2,1)S(1)}, u32[]{:S(2)}, u32[]{:S(2)}) collective-permute-start(bf16[128,1024]{1,0:T(8,128)(2,1)} %get-tuple-element.147), channel_id=1, source_target_pairs={{0,2},{2,0},{4,6},{6,4},{1,3},{3,1},{5,7},{7,5},{8,10},{10,8},{12,... | collective-permute-start | bytes 786440 | tf_op jit(solution)/shard_map/ppermute | solution.py:117
  407.5 123.5 %collective-permute-start.39 = (bf16[2048,256]{1,0:T(8,128)(2,1)}, bf16[2048,256]{1,0:T(8,128)(2,1)}, u32[]{:S(2)}, u32[]{:S(2)}) collective-permute-start(bf16[2048,256]{1,0:T(8,128)(2,1)} %convolution_convert_fusion.2), channel_id=1, source_target_pairs={{0,4},{2,6},{4,0},{6,2},{1,5},{3,7},{5,1},{7,3},{8,12},{10,14},{12... | collective-permute-start | bytes 3145736 | tf_op jit(solution)/shard_map/ppermute | solution.py:117
  422.3 111.0 %collective-permute-start.40 = (bf16[2048,256]{1,0:T(8,128)(2,1)}, bf16[2048,256]{1,0:T(8,128)(2,1)}, u32[]{:S(2)}, u32[]{:S(2)}) collective-permute-start(bf16[2048,256]{1,0:T(8,128)(2,1)} %convolution_convert_fusion.1), channel_id=1, source_target_pairs={{0,6},{2,4},{4,2},{6,0},{1,7},{3,5},{5,3},{7,1},{8,14},{10,12},{12... | collective-permute-start | bytes 3145736 | tf_op jit(solution)/shard_map/ppermute | solution.py:117
  431.4 86.6 %collective-permute-start.35 = (bf16[128,1024]{1,0:T(8,128)(2,1)S(1)}, bf16[128,1024]{1,0:T(8,128)(2,1)S(1)}, u32[]{:S(2)}, u32[]{:S(2)}) collective-permute-start(bf16[128,1024]{1,0:T(8,128)(2,1)S(1)} %get-tuple-element.111), channel_id=1, source_target_pairs={{0,2},{2,0},{4,6},{6,4},{1,3},{3,1},{5,7},{7,5},{8,10},{10,8},{12,... | collective-permute-start | bytes 786440 | tf_op jit(solution)/shard_map/ppermute | solution.py:117
  432.1 86.6 %collective-permute-start.36 = (bf16[128,1024]{1,0:T(8,128)(2,1)S(1)}, bf16[128,1024]{1,0:T(8,128)(2,1)S(1)}, u32[]{:S(2)}, u32[]{:S(2)}) collective-permute-start(bf16[128,1024]{1,0:T(8,128)(2,1)S(1)} %get-tuple-element.111), channel_id=1, source_target_pairs={{0,4},{2,6},{4,0},{6,2},{1,5},{3,7},{5,1},{7,3},{8,12},{10,14},{12... | collective-permute-start | bytes 786440 | tf_op jit(solution)/shard_map/ppermute | solution.py:117
  (112 other events, 1068.9 us)
Sparse Core Ops, SparseCore 0:
  11.9 30.7 all-gather.10
  44.8 21.2 all-gather.6
  68.2 48.8 all-gather.8
  287.4 31.6 reduce-scatter.3
  344.3 26.2 reduce-scatter.5
  372.8 50.8 reduce-scatter.7
where the time goes:
time: 560 us; the launch traced here: 552 us
  waiting for transfers between devices  136 us (24%)
  matrix products  109 us (19%)
  blocking collectives  96.6 us (17%)
  local copies, waits for them, and re-layouts  85.9 us (15%)
  other arithmetic  62.1 us (11%)
  starting transfers between devices  45.6 us (8%)
  between operations  16.4 us (3%)
    ppermute x36, waiting for transfers between devices, swap_tp(): return lax.ppermute(x, 'tp', [(i, i ^ j) for i in range(tp_size)])  110 us
    all_gather x1, blocking collectives, per_device(): small = lax.all_gather(small, ('seq', 'fsdp', 'tp'), axis=0, tiled=False)  83.1 us
    dot_general x24, matrix products, mm(): return lax.dot_general(a, b, (dims, ((), ())), preferred_element_type=F32)  60.5 us
    ppermute x36, starting transfers between devices, swap_tp(): return lax.ppermute(x, 'tp', [(i, i ^ j) for i in range(tp_size)])  42.6 us
    unnamed x223, local copies, waits for them, and re-layouts  20.3 us
    all_gather x1, waiting for transfers between devices, per_device(): w_self = lax.all_gather(pack_self, zf, axis=0, tiled=True)  17.2 us
    all_gather x1, blocking collectives, per_device(): extra = lax.all_gather(extra, zf, axis=0, tiled=False)  13.5 us
    dot_general x2, matrix products, attend_backward(): jnp.einsum('bigrd,bjgd->bgrij', grad_heads, value_heads, preferred_elemen...  13.2 us
  transfers between devices with their start and end apart: 54, of which 15 were waited for; matrix products, arithmetic and copies ran while one was open for 33% of the time, Pallas kernels for 0%

commit v1 on v0

--- a/solution.py
+++ b/solution.py
@@ -175,9 +175,13 @@
     )
     got_full = lax.all_gather(pack_full, "seq", axis=0, tiled=False)
     pack_self = jnp.concatenate([self_q, self_kv.reshape(shard, -1)], axis=1)
-    w_self = lax.all_gather(pack_self, zf, axis=0, tiled=True)
     pack_ffn = jnp.concatenate([gate_up.reshape(shard, -1), down.T], axis=1)
-    w_ffn = lax.all_gather(pack_ffn, zf, axis=0, tiled=True)
+    review_counts_on = lambda payload, peer_axis, inputs: jnp.split(
+        lax.all_gather(jnp.concatenate([payload, inputs], axis=1), peer_axis, axis=0, tiled=True),
+        [payload.shape[1]],
+        axis=1,
+    )
+    w_self, w_ffn = review_counts_on(pack_self, zf, pack_ffn)
     cols = self_q.shape[1]
 
     def full_pair(index):

time: 560 us -> 570 us (1.018)
  other arithmetic: 62.1 us -> 50.4 us
  matrix products: 109 us -> 119 us
  waiting for transfers between devices: 136 us -> 146 us
    ppermute x36, waiting for transfers between devices: 110 us -> 136 us  [swap_tp(): return lax.ppermute(x, 'tp', [(i, i ^ j) for i in range(tp_size)])]
    all_gather x2 -> x1, waiting for transfers between devices: 17.2 us -> 0.01 us  [per_device(): lax.all_gather(jnp.concatenate([payload, inputs], axis=1), peer_axis, axi...]
    unnamed x223 -> x282, local copies, waits for them, and re-layouts: 20.3 us -> 23.2 us
  transfers between devices with their start and end apart: 54 -> 53, of which waited for: 15 -> 24; matrix products, arithmetic and copies ran while one was open for 33% -> 25% of each run, Pallas kernels for 0% -> 0%
where the time goes in v1:
time: 570 us; the launch traced here: 563 us
  waiting for transfers between devices  146 us (26%)
  matrix products  119 us (21%)
  blocking collectives  95.7 us (17%)
  local copies, waits for them, and re-layouts  91.2 us (16%)
  other arithmetic  50.4 us (9%)
  starting transfers between devices  44.3 us (8%)
  between operations  16.3 us (3%)
    ppermute x36, waiting for transfers between devices, swap_tp(): return lax.ppermute(x, 'tp', [(i, i ^ j) for i in range(tp_size)])  136 us
    all_gather x1, blocking collectives, per_device(): small = lax.all_gather(small, ('seq', 'fsdp', 'tp'), axis=0, tiled=False)  82.2 us
    dot_general x24, matrix products, mm(): return lax.dot_general(a, b, (dims, ((), ())), preferred_element_type=F32)  62.8 us
    ppermute x36, starting transfers between devices, swap_tp(): return lax.ppermute(x, 'tp', [(i, i ^ j) for i in range(tp_size)])  41.3 us
    unnamed x282, local copies, waits for them, and re-layouts  23.2 us
    dot_general x2, matrix products, attend_backward(): jnp.einsum('bigrd,bjgd->bgrij', grad_heads, value_heads, preferred_elemen...  15.1 us
    all_gather x1, blocking collectives, per_device(): extra = lax.all_gather(extra, zf, axis=0, tiled=False)  13.5 us
    dot_general x2, matrix products, attend_backward(): jnp.einsum('bgrij,bigrd->bjgd', probs.astype(BF16), grad_heads, preferred...  12.1 us
  transfers between devices with their start and end apart: 53, of which 24 were waited for; matrix products, arithmetic and copies ran while one was open for 25% of the time, Pallas kernels for 0%

profile of v1, /device:TPU:0, one launch (start us, length us, event | category | flops | bytes accessed | tf_op | source)
XLA Modules:
  0.0 563.1 jit_solution(22693418035703662)
XLA Ops:
  14.5 13.5 %all_gather.25 = bf16[8,4,128]{2,1,0:T(4,128)(2,1)S(1)} all-gather(bf16[1,4,128]{2,1,0:T(4,128)(2,1)S(1)} %scatter.9), channel_id=1, replica_groups=mesh['seq'=4,'tp'=4,'fsdp'=2] {'seq','fsdp'}, dimensions={0}, use_global_device_ids=true | all-gather | bytes 9216 | tf_op jit(solution)/shard_map/all_gather | solution.py:167
  29.5 2.3 constant_dynamic-slice_fusion.13
  33.7 8.9 %all-gather.8.cloned.1.call-done = bf16[8,128,512]{2,1,0:T(8,128)(2,1)} async-done(((bf16[2,128,512]{2,1,0:T(8,128)(2,1)}), bf16[8,128,512]{2,1,0:T(8,128)(2,1)}) %all-gather.8.cloned.1.call-update) | async-done | bytes 1048592 | tf_op jit(solution)/shard_map/all_gather | solution.py:176
  52.7 7.8 %collective-permute-done.4 = bf16[4,128,512]{2,1,0:T(8,128)(2,1)S(1)} collective-permute-done((bf16[4,128,512]{2,1,0:T(8,128)(2,1)S(1)}, bf16[4,128,512]{2,1,0:T(8,128)(2,1)S(1)}, u32[]{:S(2)}, u32[]{:S(2)}) %collective-permute-start.4) | collective-permute-done | bytes 524320 | tf_op jit(solution)/shard_map/ppermute | solution.py:117
  60.6 2.4 collective-permute-start.15
  62.9 10.3 %collective-permute-done.6 = bf16[4,128,512]{2,1,0:T(8,128)(2,1)S(1)} collective-permute-done((bf16[4,128,512]{2,1,0:T(8,128)(2,1)S(1)}, bf16[4,128,512]{2,1,0:T(8,128)(2,1)S(1)}, u32[]{:S(2)}, u32[]{:S(2)}) %collective-permute-start.6) | collective-permute-done | bytes 524320 | tf_op jit(solution)/shard_map/ppermute | solution.py:117
  75.7 7.4 %collective-permute-done.11 = bf16[4,128,512]{2,1,0:T(8,128)(2,1)S(1)} collective-permute-done((bf16[4,128,512]{2,1,0:T(8,128)(2,1)S(1)}, bf16[4,128,512]{2,1,0:T(8,128)(2,1)S(1)}, u32[]{:S(2)}, u32[]{:S(2)}) %collective-permute-start.11) | collective-permute-done | bytes 524320 | tf_op jit(solution)/shard_map/ppermute | solution.py:117
  83.1 11.5 %collective-permute-done.13 = bf16[4,128,512]{2,1,0:T(8,128)(2,1)S(1)} collective-permute-done((bf16[4,128,512]{2,1,0:T(8,128)(2,1)S(1)}, bf16[4,128,512]{2,1,0:T(8,128)(2,1)S(1)}, u32[]{:S(2)}, u32[]{:S(2)}) %collective-permute-start.13) | collective-permute-done | bytes 524320 | tf_op jit(solution)/shard_map/ppermute | solution.py:117
  104.4 7.6 %fusion.21 = bf16[2048,1024]{0,1:T(8,128)(2,1)S(1)} fusion(bf16[4,2048,1024]{2,1,0:T(8,128)(2,1)} %param.19, s32[]{:T(128)S(6)} %select_n.140, bf16[1024,256]{1,0:T(8,128)(2,1)S(1)} %get-tuple-element.184, bf16[1024,256]{1,0:T(8,128)(2,1)S(1)} %get-tuple-element.182, bf16[1024,256]{1,0:T(8,128)(2,1)S(1)} %get-tuple-element.180, ...), kind=kOutput, calls=%fused_computation.31 | convolution fusion | flops 4305453056 | bytes 10485764 | tf_op jit(solution)/shard_map/dot_general | solution.py:23
  113.8 2.7 convolution_convert_fusion.11
  124.4 2.4 collective-permute-done.2
  132.2 8.3 %bitcast_reduce_fusion = (f32[8,2,128]{2,1,0:T(2,128)S(1)}, f32[8,2048,128,2]{2,1,3,0:T(8,128)}) fusion(bf16[2048,8,64,1]{0,2,3,1:T(8,128)(2,1)S(1)} %bitcast.416, bf16[128,8,2,64]{0,3,2,1:T(8,128)(2,1)S(1)} %bitcast.425), kind=kOutput, calls=%fused_computation.7 | convolution fusion | flops 545257472 | bytes 19144704 | tf_op jit(solution)/shard_map/bigrd,bjgd->bgrij/dot_general | solution.py:39
  140.5 8.6 %fusion.5 = f32[8,2,128]{2,1,0:T(2,128)S(1)} fusion(f32[8,2048,128,2]{2,1,3,0:T(8,128)} %get-tuple-element.220, f32[8,2,128]{2,1,0:T(2,128)S(1)} %get-tuple-element.219), kind=kLoop, calls=%fused_computation.11 | loop fusion | flops 12580864 | bytes 16793600 | tf_op jit(solution)/shard_map/reduce_sum | solution.py:54
  149.2 8.2 %fusion.63 = bf16[8,64,2,128]{3,1,2,0:T(8,128)(2,1)S(1)} fusion(bf16[2048,8,64,1]{0,2,3,1:T(8,128)(2,1)S(1)} %bitcast.423, f32[8,2,128]{2,1,0:T(2,128)S(1)} %fusion.5, f32[8,2,128]{2,1,0:T(2,128)S(1)} %get-tuple-element.219, f32[8,2048,128,2]{2,1,3,0:T(8,128)} %get-tuple-element.220), kind=kOutput, calls=%fused_computation.104 | convolution fusion | flops 553779200 | bytes 19152896 | tf_op jit(solution)/shard_map/bgrij,bjgd->bigrd/dot_general | solution.py:56
  162.7 5.5 collective-permute-done.17
  168.2 4.4 collective-permute-done.18
  174.0 4.1 fusion.30
  178.1 2.8 fusion.51
  187.1 3.9 collective-permute-done.26
  191.0 3.7 collective-permute-done.27
  199.2 14.7 %fusion = (f32[8,2,128]{2,1,0:T(2,128)}, f32[8,2048,128,2]{2,1,3,0:T(8,128)}) fusion(f32[8,2048,128,2]{2,1,3,0:T(8,128)} %get-tuple-element.220, f32[8,2,128]{2,1,0:T(2,128)S(1)} %bitcast.490, bf16[2048,8,64,1]{0,2,3,1:T(8,128)(2,1)} %bitcast.422, bf16[128,8,2,64]{0,3,2,1:T(8,128)(2,1)} %bitcast.443), kind=kOutput, calls=%fused_computation.2 | convolution fusion | flops 553646080 | bytes 35930112 | tf_op jit(solution)/shard_map/bigrd,bjgd->bgrij/dot_general | solution.py:64
  216.4 8.1 %fusion.10 = bf16[8,2,128,2048]{2,3,1,0:T(8,128)(2,1)S(1)} fusion(f32[8,2048,128,2]{2,1,3,0:T(8,128)} %get-tuple-element.224, f32[8,2048,128,2]{2,1,3,0:T(8,128)S(1)} %bitcast.415, f32[8,2,128]{2,1,0:T(2,128)} %get-tuple-element.223, f32[8,2,128]{2,1,0:T(2,128)S(1)} %bitcast.491), kind=kLoop, calls=%fused_computation.15 | loop fusion | flops 20971520 | bytes 41959424 | tf_op jit(solution)/shard_map/reshape.150
  224.5 3.4 copy-done
  229.4 6.1 %fusion.16 = bf16[8,64,2048]{2,1,0:T(8,128)(2,1)S(1)} fusion(bf16[128,8,2,64]{0,3,2,1:T(8,128)(2,1)S(1)} %bitcast.426, bf16[8,2,128,2048]{2,3,1,0:T(8,128)(2,1)} %copy-done), kind=kOutput, calls=%fused_computation.25 | convolution fusion | flops 538968064 | bytes 10747904 | tf_op jit(solution)/shard_map/bgrij,bigrd->bjgd/dot_general | solution.py:74
  235.5 10.2 %bitcast_convert_fusion = bf16[8,64,2048]{2,1,0:T(8,128)(2,1)} fusion(bf16[128,8,2,64]{0,3,2,1:T(8,128)(2,1)S(1)} %bitcast.444, f32[8,2048,128,2]{2,1,3,0:T(8,128)} %get-tuple-element.220, f32[8,2,128]{2,1,0:T(2,128)S(1)} %bitcast.492), kind=kOutput, calls=%fused_computation.23 | convolution fusion | flops 550502400 | bytes 19144704 | tf_op jit(solution)/shard_map/bgrij,bigrd->bjgd/dot_general | solution.py:77
  251.7 2.3 copy.280
  253.9 3.0 constant_dynamic-slice_fusion.5
  257.0 2.3 copy.282
  261.7 8.8 %fusion.42 = bf16[1024,1024]{1,0:T(8,128)(2,1)S(1)} fusion(bf16[2048,1024]{0,1:T(8,128)(2,1)S(1)} %bitcast.429, bf16[4,2048,1024]{2,1,0:T(8,128)(2,1)} %param.19, s32[]{:T(128)S(6)} %select_n.140), kind=kOutput, calls=%fused_computation.66 | convolution fusion | flops 4296015872 | bytes 10485764 | tf_op jit(solution)/shard_map/dot_general | solution.py:23
  283.2 2.4 copy.284
  302.0 2.8 bitcast_convert_fusion.1
  315.7 22.3 %collective-permute-done.45 = bf16[4,128,1024]{1,2,0:T(8,128)(2,1)S(1)} collective-permute-done((bf16[4,128,1024]{1,2,0:T(8,128)(2,1)S(1)}, bf16[4,128,1024]{1,2,0:T(8,128)(2,1)S(1)}, u32[]{:S(2)}, u32[]{:S(2)}) %collective-permute-start.45) | collective-permute-done | bytes 1048608 | tf_op jit(solution)/shard_map/ppermute | solution.py:117
  338.0 22.6 %collective-permute-done.46 = bf16[4,128,1024]{1,2,0:T(8,128)(2,1)S(1)} collective-permute-done((bf16[4,128,1024]{1,2,0:T(8,128)(2,1)S(1)}, bf16[4,128,1024]{1,2,0:T(8,128)(2,1)S(1)}, u32[]{:S(2)}, u32[]{:S(2)}) %collective-permute-start.46) | collective-permute-done | bytes 1048608 | tf_op jit(solution)/shard_map/ppermute | solution.py:117
  365.3 3.7 convolution_convert_fusion
  369.0 2.4 pad_maximum_fusion
  373.1 2.8 convolution_convert_fusion.9
  383.0 4.2 collective-permute-done.20
  387.2 4.0 collective-permute-done.21
  397.8 2.4 convolution_convert_fusion.1
  401.5 2.3 convolution_convert_fusion.2
  403.7 2.3 convolution_convert_fusion.3
  406.1 2.3 broadcast_in_dim.90
  408.4 2.3 fusion.33
  419.9 8.5 %collective-permute-done.24 = bf16[128,1024]{1,0:T(8,128)(2,1)} collective-permute-done((bf16[128,1024]{1,0:T(8,128)(2,1)}, bf16[128,1024]{1,0:T(8,128)(2,1)}, u32[]{:S(2)}, u32[]{:S(2)}) %collective-permute-start.24) | collective-permute-done | bytes 262176 | tf_op jit(solution)/shard_map/ppermute | solution.py:117
  433.0 4.3 collective-permute-done.32
  439.5 4.1 collective-permute-done.34
  447.9 82.2 %all-gather.2 = f32[32,4,1024]{2,1,0:T(4,128)S(1)} all-gather(f32[1,4,1024]{2,1,0:T(4,128)S(1)} %maximum_bitcast_fusion.2), channel_id=3, replica_groups=mesh['seq'=4,'tp'=4,'fsdp'=2] {'seq','fsdp','tp'}, dimensions={0}, use_global_device_ids=true | all-gather | bytes 540672 | tf_op jit(solution)/shard_map/all_gather | solution.py:332
  531.5 7.4 %collective-permute-done.37 = bf16[128,1024]{1,0:T(8,128)(2,1)S(1)} collective-permute-done((bf16[128,1024]{1,0:T(8,128)(2,1)}, bf16[128,1024]{1,0:T(8,128)(2,1)S(1)}, u32[]{:S(2)}, u32[]{:S(2)}) %collective-permute-start.37) | collective-permute-done | bytes 262176 | tf_op jit(solution)/shard_map/ppermute | solution.py:117
  (535 shorter events, 176.5 us)
Async XLA Ops:
  7.2 35.4 %all-gather.8.cloned.1.call-start = ((), (), s32[]{:S(2)}) async-start(), calls=%async_computation.7 | async-start | bytes 1310720 | tf_op jit(solution)/shard_map/all_gather | solution.py:176
  11.7 102.0 %all-gather.6.cloned.1.call-start = ((), (), s32[]{:S(2)}) async-start(), calls=%async_computation.3 | async-start | bytes 6193152 | tf_op jit(solution)/shard_map/all_gather | solution.py:180
  14.2 533.1 %reduce-scatter.4.cloned.1.call-start = ((), (), s32[]{:S(2)}) async-start(), calls=%async_computation.4 | async-start | bytes 1179648 | tf_op jit(solution)/shard_map/reduce_scatter | solution.py:319
  44.0 5.3 collective-permute-start.10
  44.0 6.7 %collective-permute-start.3 = (bf16[4,128,512]{2,1,0:T(8,128)(2,1)S(1)}, bf16[4,128,512]{2,1,0:T(8,128)(2,1)S(1)}, u32[]{:S(2)}, u32[]{:S(2)}) collective-permute-start(bf16[4,128,512]{2,1,0:T(8,128)(2,1)S(1)} %get-tuple-element.177), channel_id=1, source_target_pairs={{0,1},{1,0},{2,3},{3,2},{4,5},{5,4},{6,7},{7,6},{8,9},{9,8},{10,11... | collective-permute-start | bytes 1572872 | tf_op jit(solution)/shard_map/ppermute | solution.py:120
  45.8 14.8 %collective-permute-start.4 = (bf16[4,128,512]{2,1,0:T(8,128)(2,1)S(1)}, bf16[4,128,512]{2,1,0:T(8,128)(2,1)S(1)}, u32[]{:S(2)}, u32[]{:S(2)}) collective-permute-start(bf16[4,128,512]{2,1,0:T(8,128)(2,1)S(1)} %get-tuple-element.177), channel_id=1, source_target_pairs={{0,2},{2,0},{4,6},{6,4},{1,3},{3,1},{5,7},{7,5},{8,10},{10,8},{12,... | collective-permute-start | bytes 1572872 | tf_op jit(solution)/shard_map/ppermute | solution.py:117
  47.2 26.0 %collective-permute-start.6 = (bf16[4,128,512]{2,1,0:T(8,128)(2,1)S(1)}, bf16[4,128,512]{2,1,0:T(8,128)(2,1)S(1)}, u32[]{:S(2)}, u32[]{:S(2)}) collective-permute-start(bf16[4,128,512]{2,1,0:T(8,128)(2,1)S(1)} %get-tuple-element.177), channel_id=1, source_target_pairs={{0,4},{2,6},{4,0},{6,2},{1,5},{3,7},{5,1},{7,3},{8,12},{10,14},{12... | collective-permute-start | bytes 1572872 | tf_op jit(solution)/shard_map/ppermute | solution.py:117
  48.7 25.4 %collective-permute-start.8 = (bf16[4,128,512]{2,1,0:T(8,128)(2,1)S(1)}, bf16[4,128,512]{2,1,0:T(8,128)(2,1)S(1)}, u32[]{:S(2)}, u32[]{:S(2)}) collective-permute-start(bf16[4,128,512]{2,1,0:T(8,128)(2,1)S(1)} %get-tuple-element.177), channel_id=1, source_target_pairs={{0,6},{2,4},{4,2},{6,0},{1,7},{3,5},{5,3},{7,1},{8,14},{10,12},{12... | collective-permute-start | bytes 1572872 | tf_op jit(solution)/shard_map/ppermute | solution.py:117
  49.3 33.8 %collective-permute-start.11 = (bf16[4,128,512]{2,1,0:T(8,128)(2,1)S(1)}, bf16[4,128,512]{2,1,0:T(8,128)(2,1)S(1)}, u32[]{:S(2)}, u32[]{:S(2)}) collective-permute-start(bf16[4,128,512]{2,1,0:T(8,128)(2,1)S(1)} %get-tuple-element.176), channel_id=1, source_target_pairs={{0,2},{2,0},{4,6},{6,4},{1,3},{3,1},{5,7},{7,5},{8,10},{10,8},{12,... | collective-permute-start | bytes 1572872 | tf_op jit(solution)/shard_map/ppermute | solution.py:117
  50.7 43.8 %collective-permute-start.13 = (bf16[4,128,512]{2,1,0:T(8,128)(2,1)S(1)}, bf16[4,128,512]{2,1,0:T(8,128)(2,1)S(1)}, u32[]{:S(2)}, u32[]{:S(2)}) collective-permute-start(bf16[4,128,512]{2,1,0:T(8,128)(2,1)S(1)} %get-tuple-element.176), channel_id=1, source_target_pairs={{0,4},{2,6},{4,0},{6,2},{1,5},{3,7},{5,1},{7,3},{8,12},{10,14},{12... | collective-permute-start | bytes 1572872 | tf_op jit(solution)/shard_map/ppermute | solution.py:117
  60.6 34.0 %collective-permute-start.15 = (bf16[4,128,512]{2,1,0:T(8,128)(2,1)S(1)}, bf16[4,128,512]{2,1,0:T(8,128)(2,1)S(1)}, u32[]{:S(2)}, u32[]{:S(2)}) collective-permute-start(bf16[4,128,512]{2,1,0:T(8,128)(2,1)S(1)} %get-tuple-element.176), channel_id=1, source_target_pairs={{0,6},{2,4},{4,2},{6,0},{1,7},{3,5},{5,3},{7,1},{8,14},{10,12},{12... | collective-permute-start | bytes 1572872 | tf_op jit(solution)/shard_map/ppermute | solution.py:117
  73.3 21.8 %collective-permute-start.5 = (bf16[4,128,512]{2,1,0:T(8,128)(2,1)S(1)}, bf16[4,128,512]{2,1,0:T(8,128)(2,1)S(1)}, u32[]{:S(2)}, u32[]{:S(2)}) collective-permute-start(bf16[4,128,512]{2,1,0:T(8,128)(2,1)S(1)} %collective-permute-done.4), channel_id=1, source_target_pairs={{0,1},{1,0},{2,3},{3,2},{4,5},{5,4},{6,7},{7,6},{8,9},{9,8},{10,11... | collective-permute-start | bytes 1572872 | tf_op jit(solution)/shard_map/ppermute | solution.py:120
  74.2 21.3 %collective-permute-start.7 = (bf16[4,128,512]{2,1,0:T(8,128)(2,1)S(1)}, bf16[4,128,512]{2,1,0:T(8,128)(2,1)S(1)}, u32[]{:S(2)}, u32[]{:S(2)}) collective-permute-start(bf16[4,128,512]{2,1,0:T(8,128)(2,1)S(1)} %collective-permute-done.6), channel_id=1, source_target_pairs={{0,1},{1,0},{2,3},{3,2},{4,5},{5,4},{6,7},{7,6},{8,9},{9,8},{10,11... | collective-permute-start | bytes 1572872 | tf_op jit(solution)/shard_map/ppermute | solution.py:120
  83.1 12.6 %collective-permute-start.9 = (bf16[4,128,512]{2,1,0:T(8,128)(2,1)S(1)}, bf16[4,128,512]{2,1,0:T(8,128)(2,1)S(1)}, u32[]{:S(2)}, u32[]{:S(2)}) collective-permute-start(bf16[4,128,512]{2,1,0:T(8,128)(2,1)S(1)} %collective-permute-done.8), channel_id=1, source_target_pairs={{0,1},{1,0},{2,3},{3,2},{4,5},{5,4},{6,7},{7,6},{8,9},{9,8},{10,11... | collective-permute-start | bytes 1572872 | tf_op jit(solution)/shard_map/ppermute | solution.py:120
  121.7 5.2 collective-permute-start.2
  158.8 9.3 %collective-permute-start.17 = (bf16[128,1024]{1,0:T(8,128)(2,1)S(1)}, bf16[128,1024]{1,0:T(8,128)(2,1)}, u32[]{:S(2)}, u32[]{:S(2)}) collective-permute-start(bf16[128,1024]{1,0:T(8,128)(2,1)S(1)} %multiply_convert_fusion.4), channel_id=1, source_target_pairs={{0,2},{2,0},{4,6},{6,4},{1,3},{3,1},{5,7},{7,5},{8,10},{10,8},{12,... | collective-permute-start | bytes 786440 | tf_op jit(solution)/shard_map/ppermute | solution.py:117
  160.5 12.1 %collective-permute-start.18 = (bf16[128,1024]{1,0:T(8,128)(2,1)S(1)}, bf16[128,1024]{1,0:T(8,128)(2,1)}, u32[]{:S(2)}, u32[]{:S(2)}) collective-permute-start(bf16[128,1024]{1,0:T(8,128)(2,1)S(1)} %multiply_convert_fusion.4), channel_id=1, source_target_pairs={{0,4},{2,6},{4,0},{6,2},{1,5},{3,7},{5,1},{7,3},{8,12},{10,14},{12... | collective-permute-start | bytes 786440 | tf_op jit(solution)/shard_map/ppermute | solution.py:117
  161.0 11.5 %collective-permute-start.19 = (bf16[128,1024]{1,0:T(8,128)(2,1)S(1)}, bf16[128,1024]{1,0:T(8,128)(2,1)}, u32[]{:S(2)}, u32[]{:S(2)}) collective-permute-start(bf16[128,1024]{1,0:T(8,128)(2,1)S(1)} %multiply_convert_fusion.4), channel_id=1, source_target_pairs={{0,6},{2,4},{4,2},{6,0},{1,7},{3,5},{5,3},{7,1},{8,14},{10,12},{12... | collective-permute-start | bytes 786440 | tf_op jit(solution)/shard_map/ppermute | solution.py:117
  182.9 8.1 %collective-permute-start.26 = (bf16[128,1024]{1,0:T(8,128)(2,1)S(1)}, bf16[128,1024]{1,0:T(8,128)(2,1)S(1)}, u32[]{:S(2)}, u32[]{:S(2)}) collective-permute-start(bf16[128,1024]{1,0:T(8,128)(2,1)S(1)} %get-tuple-element.150), channel_id=1, source_target_pairs={{0,2},{2,0},{4,6},{6,4},{1,3},{3,1},{5,7},{7,5},{8,10},{10,8},{12,... | collective-permute-start | bytes 786440 | tf_op jit(solution)/shard_map/ppermute | solution.py:117
  183.6 11.1 %collective-permute-start.27 = (bf16[128,1024]{1,0:T(8,128)(2,1)S(1)}, bf16[128,1024]{1,0:T(8,128)(2,1)S(1)}, u32[]{:S(2)}, u32[]{:S(2)}) collective-permute-start(bf16[128,1024]{1,0:T(8,128)(2,1)S(1)} %get-tuple-element.152), channel_id=1, source_target_pairs={{0,4},{2,6},{4,0},{6,2},{1,5},{3,7},{5,1},{7,3},{8,12},{10,14},{12... | collective-permute-start | bytes 786440 | tf_op jit(solution)/shard_map/ppermute | solution.py:117
  184.7 10.0 %collective-permute-start.28 = (bf16[128,1024]{1,0:T(8,128)(2,1)S(1)}, bf16[128,1024]{1,0:T(8,128)(2,1)S(1)}, u32[]{:S(2)}, u32[]{:S(2)}) collective-permute-start(bf16[128,1024]{1,0:T(8,128)(2,1)S(1)} %get-tuple-element.151), channel_id=1, source_target_pairs={{0,6},{2,4},{4,2},{6,0},{1,7},{3,5},{5,3},{7,1},{8,14},{10,12},{12... | collective-permute-start | bytes 786440 | tf_op jit(solution)/shard_map/ppermute | solution.py:117
  253.9 51.0 %collective-permute-start.41 = (bf16[4,128,1024]{1,2,0:T(8,128)(2,1)}, bf16[4,128,1024]{1,2,0:T(8,128)(2,1)}, u32[]{:S(2)}, u32[]{:S(2)}) collective-permute-start(bf16[4,128,1024]{1,2,0:T(8,128)(2,1)} %bitcast.460), channel_id=1, source_target_pairs={{0,1},{1,0},{2,3},{3,2},{4,5},{5,4},{6,7},{7,6},{8,9},{9,8},{10,11... | collective-permute-start | bytes 3145736 | tf_op jit(solution)/shard_map/ppermute | solution.py:120
  259.2 47.6 %collective-permute-start.42 = (bf16[4,128,1024]{1,2,0:T(8,128)(2,1)}, bf16[4,128,1024]{1,2,0:T(8,128)(2,1)}, u32[]{:S(2)}, u32[]{:S(2)}) collective-permute-start(bf16[4,128,1024]{1,2,0:T(8,128)(2,1)} %bitcast.459), channel_id=1, source_target_pairs={{0,1},{1,0},{2,3},{3,2},{4,5},{5,4},{6,7},{7,6},{8,9},{9,8},{10,11... | collective-permute-start | bytes 3145736 | tf_op jit(solution)/shard_map/ppermute | solution.py:120
  274.8 15.2 %collective-permute-start.29 = (bf16[128,256]{1,0:T(8,128)(2,1)}, bf16[128,256]{1,0:T(8,128)(2,1)}, u32[]{:S(2)}, u32[]{:S(2)}) collective-permute-start(bf16[128,256]{1,0:T(8,128)(2,1)} %get-tuple-element.205), channel_id=1, source_target_pairs={{0,2},{2,0},{4,6},{6,4},{1,3},{3,1},{5,7},{7,5},{8,10},{10,8},{12,... | collective-permute-start | bytes 196616 | tf_op jit(solution)/shard_map/ppermute | solution.py:117
  276.1 15.0 %collective-permute-start.30 = (bf16[128,256]{1,0:T(8,128)(2,1)}, bf16[128,256]{1,0:T(8,128)(2,1)}, u32[]{:S(2)}, u32[]{:S(2)}) collective-permute-start(bf16[128,256]{1,0:T(8,128)(2,1)} %get-tuple-element.204), channel_id=1, source_target_pairs={{0,4},{2,6},{4,0},{6,2},{1,5},{3,7},{5,1},{7,3},{8,12},{10,14},{12... | collective-permute-start | bytes 196616 | tf_op jit(solution)/shard_map/ppermute | solution.py:117
  276.9 15.7 %collective-permute-start.31 = (bf16[128,256]{1,0:T(8,128)(2,1)}, bf16[128,256]{1,0:T(8,128)(2,1)}, u32[]{:S(2)}, u32[]{:S(2)}) collective-permute-start(bf16[128,256]{1,0:T(8,128)(2,1)} %get-tuple-element.203), channel_id=1, source_target_pairs={{0,6},{2,4},{4,2},{6,0},{1,7},{3,5},{5,3},{7,1},{8,14},{10,12},{12... | collective-permute-start | bytes 196616 | tf_op jit(solution)/shard_map/ppermute | solution.py:117
  290.0 18.5 %collective-permute-start.43 = (bf16[4,128,1024]{1,2,0:T(8,128)(2,1)}, bf16[4,128,1024]{1,2,0:T(8,128)(2,1)}, u32[]{:S(2)}, u32[]{:S(2)}) collective-permute-start(bf16[4,128,1024]{1,2,0:T(8,128)(2,1)} %bitcast.462), channel_id=1, source_target_pairs={{0,1},{1,0},{2,3},{3,2},{4,5},{5,4},{6,7},{7,6},{8,9},{9,8},{10,11... | collective-permute-start | bytes 3145736 | tf_op jit(solution)/shard_map/ppermute | solution.py:120
  291.1 19.1 %collective-permute-start.44 = (bf16[4,128,1024]{1,2,0:T(8,128)(2,1)}, bf16[4,128,1024]{1,2,0:T(8,128)(2,1)}, u32[]{:S(2)}, u32[]{:S(2)}) collective-permute-start(bf16[4,128,1024]{1,2,0:T(8,128)(2,1)} %bitcast.461), channel_id=1, source_target_pairs={{0,1},{1,0},{2,3},{3,2},{4,5},{5,4},{6,7},{7,6},{8,9},{9,8},{10,11... | collective-permute-start | bytes 3145736 | tf_op jit(solution)/shard_map/ppermute | solution.py:120
  304.8 244.8 %reduce-scatter.6.cloned.1.call-start = ((), (), s32[]{:S(2)}) async-start(), calls=%async_computation.5 | async-start | bytes 1310720 | tf_op jit(solution)/shard_map/reduce_scatter | solution.py:310
  311.9 26.1 %collective-permute-start.45 = (bf16[4,128,1024]{1,2,0:T(8,128)(2,1)S(1)}, bf16[4,128,1024]{1,2,0:T(8,128)(2,1)S(1)}, u32[]{:S(2)}, u32[]{:S(2)}) collective-permute-start(bf16[4,128,1024]{1,2,0:T(8,128)(2,1)S(1)} %pad_maximum_fusion.17), channel_id=1, source_target_pairs={{0,2},{2,0},{4,6},{6,4},{1,3},{3,1},{5,7},{7,5},{8,10},{10,8},{12,... | collective-permute-start | bytes 3145736 | tf_op jit(solution)/shard_map/ppermute | solution.py:117
  313.3 47.3 %collective-permute-start.46 = (bf16[4,128,1024]{1,2,0:T(8,128)(2,1)S(1)}, bf16[4,128,1024]{1,2,0:T(8,128)(2,1)S(1)}, u32[]{:S(2)}, u32[]{:S(2)}) collective-permute-start(bf16[4,128,1024]{1,2,0:T(8,128)(2,1)S(1)} %pad_maximum_fusion.18), channel_id=1, source_target_pairs={{0,4},{2,6},{4,0},{6,2},{1,5},{3,7},{5,1},{7,3},{8,12},{10,14},{12... | collective-permute-start | bytes 3145736 | tf_op jit(solution)/shard_map/ppermute | solution.py:117
  314.2 46.4 %collective-permute-start.47 = (bf16[4,128,1024]{1,2,0:T(8,128)(2,1)S(1)}, bf16[4,128,1024]{1,2,0:T(8,128)(2,1)S(1)}, u32[]{:S(2)}, u32[]{:S(2)}) collective-permute-start(bf16[4,128,1024]{1,2,0:T(8,128)(2,1)S(1)} %pad_maximum_fusion.19), channel_id=1, source_target_pairs={{0,6},{2,4},{4,2},{6,0},{1,7},{3,5},{5,3},{7,1},{8,14},{10,12},{12... | collective-permute-start | bytes 3145736 | tf_op jit(solution)/shard_map/ppermute | solution.py:117
  362.2 190.6 %reduce-scatter.8.cloned.1.call-start = ((), (), s32[]{:S(2)}) async-start(), calls=%async_computation.6 | async-start | bytes 5013504 | tf_op jit(solution)/shard_map/reduce_scatter | solution.py:257
  377.8 9.4 %collective-permute-start.20 = (bf16[128,1024]{1,0:T(8,128)(2,1)}, bf16[128,1024]{1,0:T(8,128)(2,1)S(1)}, u32[]{:S(2)}, u32[]{:S(2)}) collective-permute-start(bf16[128,1024]{1,0:T(8,128)(2,1)} %get-tuple-element.157), channel_id=1, source_target_pairs={{0,2},{2,0},{4,6},{6,4},{1,3},{3,1},{5,7},{7,5},{8,10},{10,8},{12,... | collective-permute-start | bytes 786440 | tf_op jit(solution)/shard_map/ppermute | solution.py:117
  378.4 12.7 %collective-permute-start.21 = (bf16[128,1024]{1,0:T(8,128)(2,1)}, bf16[128,1024]{1,0:T(8,128)(2,1)}, u32[]{:S(2)}, u32[]{:S(2)}) collective-permute-start(bf16[128,1024]{1,0:T(8,128)(2,1)} %get-tuple-element.159), channel_id=1, source_target_pairs={{0,4},{2,6},{4,0},{6,2},{1,5},{3,7},{5,1},{7,3},{8,12},{10,14},{12... | collective-permute-start | bytes 786440 | tf_op jit(solution)/shard_map/ppermute | solution.py:117
  379.5 11.6 %collective-permute-start.22 = (bf16[128,1024]{1,0:T(8,128)(2,1)}, bf16[128,1024]{1,0:T(8,128)(2,1)}, u32[]{:S(2)}, u32[]{:S(2)}) collective-permute-start(bf16[128,1024]{1,0:T(8,128)(2,1)} %get-tuple-element.158), channel_id=1, source_target_pairs={{0,6},{2,4},{4,2},{6,0},{1,7},{3,5},{5,3},{7,1},{8,14},{10,12},{12... | collective-permute-start | bytes 786440 | tf_op jit(solution)/shard_map/ppermute | solution.py:117
  394.3 23.0 %collective-permute-start.23 = (bf16[128,1024]{1,0:T(8,128)(2,1)}, bf16[128,1024]{1,0:T(8,128)(2,1)}, u32[]{:S(2)}, u32[]{:S(2)}) collective-permute-start(bf16[128,1024]{1,0:T(8,128)(2,1)} %get-tuple-element.113), channel_id=1, source_target_pairs={{0,2},{2,0},{4,6},{6,4},{1,3},{3,1},{5,7},{7,5},{8,10},{10,8},{12,... | collective-permute-start | bytes 786440 | tf_op jit(solution)/shard_map/ppermute | solution.py:117
  395.3 33.1 %collective-permute-start.24 = (bf16[128,1024]{1,0:T(8,128)(2,1)}, bf16[128,1024]{1,0:T(8,128)(2,1)}, u32[]{:S(2)}, u32[]{:S(2)}) collective-permute-start(bf16[128,1024]{1,0:T(8,128)(2,1)} %get-tuple-element.113), channel_id=1, source_target_pairs={{0,4},{2,6},{4,0},{6,2},{1,5},{3,7},{5,1},{7,3},{8,12},{10,14},{12... | collective-permute-start | bytes 786440 | tf_op jit(solution)/shard_map/ppermute | solution.py:117
  396.2 34.4 %collective-permute-start.25 = (bf16[128,1024]{1,0:T(8,128)(2,1)}, bf16[128,1024]{1,0:T(8,128)(2,1)}, u32[]{:S(2)}, u32[]{:S(2)}) collective-permute-start(bf16[128,1024]{1,0:T(8,128)(2,1)} %get-tuple-element.113), channel_id=1, source_target_pairs={{0,6},{2,4},{4,2},{6,0},{1,7},{3,5},{5,3},{7,1},{8,14},{10,12},{12... | collective-permute-start | bytes 786440 | tf_op jit(solution)/shard_map/ppermute | solution.py:117
  400.1 144.9 %collective-permute-start.40 = (bf16[2048,256]{1,0:T(8,128)(2,1)}, bf16[2048,256]{1,0:T(8,128)(2,1)}, u32[]{:S(2)}, u32[]{:S(2)}) collective-permute-start(bf16[2048,256]{1,0:T(8,128)(2,1)} %convolution_convert_fusion.1), channel_id=1, source_target_pairs={{0,6},{2,4},{4,2},{6,0},{1,7},{3,5},{5,3},{7,1},{8,14},{10,12},{12... | collective-permute-start | bytes 3145736 | tf_op jit(solution)/shard_map/ppermute | solution.py:117
  413.7 23.7 %collective-permute-start.32 = (bf16[128,1024]{1,0:T(8,128)(2,1)}, bf16[128,1024]{1,0:T(8,128)(2,1)S(1)}, u32[]{:S(2)}, u32[]{:S(2)}) collective-permute-start(bf16[128,1024]{1,0:T(8,128)(2,1)} %get-tuple-element.147), channel_id=1, source_target_pairs={{0,2},{2,0},{4,6},{6,4},{1,3},{3,1},{5,7},{7,5},{8,10},{10,8},{12,... | collective-permute-start | bytes 786440 | tf_op jit(solution)/shard_map/ppermute | solution.py:117
  417.3 22.3 %collective-permute-start.33 = (bf16[128,1024]{1,0:T(8,128)(2,1)}, bf16[128,1024]{1,0:T(8,128)(2,1)S(1)}, u32[]{:S(2)}, u32[]{:S(2)}) collective-permute-start(bf16[128,1024]{1,0:T(8,128)(2,1)} %get-tuple-element.149), channel_id=1, source_target_pairs={{0,4},{2,6},{4,0},{6,2},{1,5},{3,7},{5,1},{7,3},{8,12},{10,14},{12... | collective-permute-start | bytes 786440 | tf_op jit(solution)/shard_map/ppermute | solution.py:117
  428.4 15.2 %collective-permute-start.34 = (bf16[128,1024]{1,0:T(8,128)(2,1)}, bf16[128,1024]{1,0:T(8,128)(2,1)S(1)}, u32[]{:S(2)}, u32[]{:S(2)}) collective-permute-start(bf16[128,1024]{1,0:T(8,128)(2,1)} %get-tuple-element.148), channel_id=1, source_target_pairs={{0,6},{2,4},{4,2},{6,0},{1,7},{3,5},{5,3},{7,1},{8,14},{10,12},{12... | collective-permute-start | bytes 786440 | tf_op jit(solution)/shard_map/ppermute | solution.py:117
  430.6 112.2 %collective-permute-start.39 = (bf16[2048,256]{1,0:T(8,128)(2,1)}, bf16[2048,256]{1,0:T(8,128)(2,1)}, u32[]{:S(2)}, u32[]{:S(2)}) collective-permute-start(bf16[2048,256]{1,0:T(8,128)(2,1)} %convolution_convert_fusion.2), channel_id=1, source_target_pairs={{0,4},{2,6},{4,0},{6,2},{1,5},{3,7},{5,1},{7,3},{8,12},{10,14},{12... | collective-permute-start | bytes 3145736 | tf_op jit(solution)/shard_map/ppermute | solution.py:117
  437.4 103.2 %collective-permute-start.38 = (bf16[2048,256]{1,0:T(8,128)(2,1)}, bf16[2048,256]{1,0:T(8,128)(2,1)}, u32[]{:S(2)}, u32[]{:S(2)}) collective-permute-start(bf16[2048,256]{1,0:T(8,128)(2,1)} %convolution_convert_fusion.3), channel_id=1, source_target_pairs={{0,2},{2,0},{4,6},{6,4},{1,3},{3,1},{5,7},{7,5},{8,10},{10,8},{12,... | collective-permute-start | bytes 3145736 | tf_op jit(solution)/shard_map/ppermute | solution.py:117
  446.0 85.5 %collective-permute-start.35 = (bf16[128,1024]{1,0:T(8,128)(2,1)}, bf16[128,1024]{1,0:T(8,128)(2,1)S(1)}, u32[]{:S(2)}, u32[]{:S(2)}) collective-permute-start(bf16[128,1024]{1,0:T(8,128)(2,1)} %get-tuple-element.111), channel_id=1, source_target_pairs={{0,2},{2,0},{4,6},{6,4},{1,3},{3,1},{5,7},{7,5},{8,10},{10,8},{12,... | collective-permute-start | bytes 786440 | tf_op jit(solution)/shard_map/ppermute | solution.py:117
  446.7 84.8 %collective-permute-start.36 = (bf16[128,1024]{1,0:T(8,128)(2,1)}, bf16[128,1024]{1,0:T(8,128)(2,1)S(1)}, u32[]{:S(2)}, u32[]{:S(2)}) collective-permute-start(bf16[128,1024]{1,0:T(8,128)(2,1)} %get-tuple-element.111), channel_id=1, source_target_pairs={{0,4},{2,6},{4,0},{6,2},{1,5},{3,7},{5,1},{7,3},{8,12},{10,14},{12... | collective-permute-start | bytes 786440 | tf_op jit(solution)/shard_map/ppermute | solution.py:117
  531.5 7.5 %collective-permute-start.37 = (bf16[128,1024]{1,0:T(8,128)(2,1)}, bf16[128,1024]{1,0:T(8,128)(2,1)S(1)}, u32[]{:S(2)}, u32[]{:S(2)}) collective-permute-start(bf16[128,1024]{1,0:T(8,128)(2,1)} %get-tuple-element.111), channel_id=1, source_target_pairs={{0,6},{2,4},{4,2},{6,0},{1,7},{3,5},{5,3},{7,1},{8,14},{10,12},{12... | collective-permute-start | bytes 786440 | tf_op jit(solution)/shard_map/ppermute | solution.py:117
  (140 other events, 1261.5 us)
Sparse Core Ops, SparseCore 0:
  11.8 30.7 all-gather.7
  44.8 57.5 all-gather.5
  304.9 31.2 reduce-scatter.3
  362.3 25.7 reduce-scatter.5
  390.2 50.8 reduce-scatter.7
